TPU v7x, 256 devices: a whole 4x4x8 slice. The times are simulated.
256 devices in a mesh: section: 4 (over x_hi, core), tp: 2 (over x_lo), doc: 32 (over z, y).
Axes of the slice: x: 4 (x_hi: 2, x_lo: 2; x = x_hi * 2 + x_lo), y: 4, z: 8, core: 2. Of those that a mesh axis runs over, the one named last changes fastest.
Arguments:
- token_ids: int32 [64, 2, 32], P('doc'), may hold values from 0 to 16383
- seg_lengths: int32 [64, 2], P('doc'), may hold values from 1 to 32
- emb_table: bfloat16 [16384, 4096], P('section', 'tp'), may hold values from -6 to 6
- mem_init: bfloat16 [16, 4096], P(None, 'tp'), may hold values from -6 to 6
- norm_gain: float32 [4, 4096], P('section'), may hold values from 0.1 to 1.9
- w_query: bfloat16 [4, 4096, 2048], P('section', 'doc', 'tp'), may hold values from -0.09375 to 0.09375
- w_key: bfloat16 [4, 4096, 2048], P('section', 'doc', 'tp'), may hold values from -0.09375 to 0.09375
- w_value: bfloat16 [4, 4096, 2048], P('section', 'doc', 'tp'), may hold values from -0.09375 to 0.09375
- w_out: bfloat16 [4, 2048, 4096], P('section', None, 'tp'), may hold values from -0.125 to 0.125
- layer_mix: float32 [4], P('section'), may hold values from 0.5 to 4.5
Outputs:
- pooled: float32 [64, 4096], P(None, 'tp')
All inputs are finite; a program needn't handle non-finite values.
Results may differ from a plain program's by a relative error of at most 0.013.
Values may be sent and summed in bfloat16 or wider, within the bound.
A program may use at most 192 MiB of HBM per device.

v0:
```python
import math

import jax
import jax.numpy as jnp
from jax import lax
from jax.sharding import PartitionSpec as P

HD = 128
M = 16
L = 32
SEGS = 2


EPSILON = 1e-05
NEGATIVE = -1e30


def side_by_side(arrays, axis, dim, along):
    widths = [a.shape[along] for a in arrays]
    both = jnp.concatenate(arrays, axis=along)
    out = lax.all_gather(both, axis, axis=dim, tiled=True)
    return tuple(jnp.split(out, [sum(widths[:k]) for k in range(1, len(widths))], axis=along))


def from_behind(block, axis, distance):
    devices = range(lax.axis_size(axis))
    route = [((i - distance) % len(devices), i) for i in devices]
    return lax.ppermute(block, axis, route)


def laid_out(parts, dim):
    lengths = list(parts.shape[1:])
    lengths[dim] *= parts.shape[0]
    return jnp.moveaxis(parts, 0, dim).reshape(lengths)


def copy_for_each(shard, axis):
    copies = jnp.broadcast_to(shard, (lax.axis_size(axis), *shard.shape))
    return lax.all_to_all(copies, axis, split_axis=0, concat_axis=0, tiled=True)


def collect(shard, axis, dim):
    return laid_out(copy_for_each(shard, axis), dim)


def visible_rows(row_count, length):
    position = jnp.arange(row_count)
    key_ok = (position < M) | (position - M < length)
    ordered = (
        (position[None, :] < M) | (position[:, None] < M) | (position[None, :] <= position[:, None])
    )
    return key_ok[None, :] & ordered


def attend(features, length, query_proj, key_proj, value_proj, norm_row):
    row_count = features.shape[0]
    local_heads = query_proj.shape[1] // HD
    floats = features.astype(jnp.float32)
    mean_square = jnp.mean(floats * floats, -1, keepdims=True)
    normed = (floats * lax.rsqrt(mean_square + EPSILON) * norm_row).astype(jnp.bfloat16)
    head_shape = (row_count, local_heads, HD)
    queries = (
        jnp.dot(normed, query_proj, preferred_element_type=jnp.float32)
        .astype(jnp.bfloat16)
        .reshape(head_shape)
    )
    keys = (
        jnp.dot(normed, key_proj, preferred_element_type=jnp.float32)
        .astype(jnp.bfloat16)
        .reshape(head_shape)
    )
    values = (
        jnp.dot(normed, value_proj, preferred_element_type=jnp.float32)
        .astype(jnp.bfloat16)
        .reshape(head_shape)
    )
    scores = jnp.einsum("qhe,khe->hqk", queries, keys, preferred_element_type=jnp.float32) * (
        1.0 / math.sqrt(HD)
    )
    allowed = visible_rows(row_count, length)[None]
    scores = jnp.where(allowed, scores, NEGATIVE)
    weights = jnp.where(allowed, jnp.exp(scores), 0.0)
    probs = (weights / jnp.sum(weights, -1, keepdims=True)).astype(jnp.bfloat16)
    mixed = jnp.einsum("hqk,khe->qhe", probs, values, preferred_element_type=jnp.float32).astype(
        jnp.bfloat16
    )
    return mixed.reshape(row_count, local_heads * HD)


def body(
    token_ids,
    seg_lengths,
    emb_table,
    mem_init,
    norm_gain,
    w_query,
    w_key,
    w_value,
    w_out,
    layer_mix,
):
    phases = lax.axis_size("section")
    phase_index = lax.axis_index("section")
    doc_local = token_ids.shape[0]
    vocab_rows = emb_table.shape[0]
    width_local = emb_table.shape[1]
    flat_ids = token_ids.reshape(-1)
    local_ids = flat_ids - phase_index * vocab_rows
    owned = (local_ids >= 0) & (local_ids < vocab_rows)
    picked_rows = jnp.take(emb_table, jnp.clip(local_ids, 0, vocab_rows - 1), axis=0)
    partial_rows = jnp.where(owned[:, None], picked_rows.astype(jnp.float32), 0.0)
    embedded = lax.psum(partial_rows.astype(jnp.bfloat16), "section")
    embedded = embedded.reshape(doc_local * SEGS, L, width_local)
    query_proj, key_proj, value_proj = side_by_side((w_query[0], w_key[0], w_value[0]), "doc", 0, 1)
    out_proj = w_out[0]
    norm_row = norm_gain[0]
    mixing = layer_mix[0]
    row_count = M + L
    head_cols = query_proj.shape[1]
    total_turns = (SEGS - 1) * phases + doc_local + phases - 1

    def turn(turn_index, carried):
        incoming, returned, pooled = carried
        offset = turn_index - phase_index
        segment = offset // phases
        document = offset % phases
        active = (offset >= 0) & (document < doc_local) & (segment < SEGS)
        segment = jnp.clip(segment, 0, SEGS - 1)
        document = jnp.clip(document, 0, doc_local - 1)
        tokens = lax.dynamic_index_in_dim(embedded, document * SEGS + segment, 0, keepdims=False)
        earlier = incoming[:M]
        memory = jnp.where(segment == 0, mem_init, earlier)
        hidden = jnp.where(phase_index == 0, jnp.concatenate([memory, tokens], 0), incoming)
        length = seg_lengths[document, segment]
        features = lax.all_gather(hidden, "tp", axis=1, tiled=True)
        heads_out = lax.cond(
            active,
            lambda: attend(features, length, query_proj, key_proj, value_proj, norm_row),
            lambda: jnp.zeros((row_count, head_cols), jnp.bfloat16),
        )
        every_head = lax.all_gather(heads_out, "tp", axis=1, tiled=True)
        update = lax.cond(
            active,
            lambda: jnp.dot(every_head, out_proj, preferred_element_type=jnp.float32),
            lambda: jnp.zeros((row_count, width_local), jnp.float32),
        )
        result = (hidden.astype(jnp.float32) + update).astype(jnp.bfloat16)
        token_ok = jnp.arange(L) < length
        summed = jnp.sum(
            jnp.where(token_ok[:, None], result[M:].astype(jnp.float32), 0.0), 0
        ) / length.astype(jnp.float32)
        scale_now = jnp.where(active & (segment == SEGS - 1), mixing, 0.0)
        picked = (jnp.arange(doc_local) == document).astype(jnp.float32)
        pooled = pooled + picked[:, None] * (scale_now * summed)[None, :]
        incoming = from_behind(result, "section", 1)
        return (incoming, returned, pooled)

    start_state = (
        jnp.zeros((row_count, width_local), jnp.bfloat16),
        jnp.zeros((M, width_local), jnp.bfloat16),
        jnp.zeros((doc_local, width_local), jnp.float32),
    )
    final_state = lax.fori_loop(0, total_turns, turn, start_state)
    pooled = final_state[2]
    layer_total = lax.psum(pooled, "section")
    return collect(layer_total, "doc", 0)


def solution(mesh):
    return jax.shard_map(
        body,
        mesh=mesh,
        in_specs=(
            P("doc", None, None),
            P("doc", None),
            P("section", "tp"),
            P(None, "tp"),
            P("section", None),
            P("section", "doc", "tp"),
            P("section", "doc", "tp"),
            P("section", "doc", "tp"),
            P("section", None, "tp"),
            P("section"),
        ),
        out_specs=P(None, "tp"),
        check_vma=False,
    )
```

profile of v0, /device:TPU:1, one launch (start us, length us, event | category | flops | bytes accessed | tf_op | source)
XLA Modules:
  0.0 538.9 jit_solution(7246789136166503386)
XLA Ops:
  11.2 9.4 %gather_fusion = bf16[128,2048]{1,0:T(8,128)(2,1)S(1)} fusion(bf16[4096,2048]{1,0:T(8,128)(2,1)} %param.18, s32[1024]{0:T(1024)S(1)} %pad_clamp_fusion), kind=kCustom, calls=%fused_computation | custom fusion | bytes 1049088 | tf_op jit(solution)/shard_map/jit(_take)/gather | solution.py:110
  21.8 175.6 %all-gather.2.cloned.1.call-done = bf16[4096,3072]{1,0:T(8,128)(2,1)} async-done(((bf16[128,3072]{1,0:T(8,128)(2,1)}), bf16[4096,3072]{1,0:T(8,128)(2,1)}) %all-gather.2.cloned.1.call-update) | async-done | bytes 25165840 | tf_op jit(solution)/shard_map/all_gather | solution.py:21
  197.3 16.9 %fusion.25 = (bf16[4096,1024]{1,0:T(8,128)(2,1)}, bf16[4096,1024]{1,0:T(8,128)(2,1)}, bf16[4096,1024]{1,0:T(8,128)(2,1)}) fusion(bf16[4096,3072]{1,0:T(8,128)(2,1)} %all-gather.2.cloned.1.call-done), kind=kLoop, calls=%fused_computation.52 | loop fusion | bytes 50331648 | tf_op jit(solution)/shard_map/split | solution.py:22
  214.3 280.4 %while.18 = (s32[]{:T(128)}, bf16[48,2048]{1,0:T(8,128)(2,1)S(1)}, f32[2,2048]{1,0:T(2,128)S(1)}, pred[]{:T(512)}, s32[]{:T(128)}, /*index=5*/bf16[16,2048]{1,0:...) while((s32[]{:T(128)}, bf16[48,2048]{1,0:T(8,128)(2,1)S(1)}, ...), condition=%wide.region_9.10_spmd.clone, body=%wide.region_1.9_spmd.clone.sunk | while | flops 1624327808 | bytes 90839752 | solution.py:163
  215.4 5.7 %all_gather.28 = bf16[48,4096]{1,0:T(8,128)(2,1)S(1)} all-gather(bf16[48,2048]{1,0:T(8,128)(2,1)S(1)} %maximum_select_fusion.2), channel_id=1, replica_groups=mesh['section'=4,'tp'=2,'doc'=32] {'tp'}, dimensions={1}, use_global_device_ids=true | all-gather | bytes 589824 | tf_op jit(solution)/shard_map/while/body/eval_jaxpr/all_gather | solution.py:135
  226.0 6.1 %collective-permute-start = (bf16[48,2048]{1,0:T(8,128)(2,1)S(1)}, bf16[48,2048]{1,0:T(8,128)(2,1)S(1)}, u32[]{:S(2)}, u32[]{:S(2)}) collective-permute-start(bf16[48,2048]{1,0:T(8,128)(2,1)S(1)} %add_convert_fusion.2), channel_id=1, source_target_pairs={{192,0},{0,64},{64,128},{128,192},{193,1},{1,65},{65,129},{129,193... | collective-permute-start | bytes 589832 | tf_op jit(solution)/shard_map/while/body/eval_jaxpr/ppermute | solution.py:28
  234.2 11.5 %collective-permute-done = bf16[48,2048]{1,0:T(8,128)(2,1)S(1)} collective-permute-done((bf16[48,2048]{1,0:T(8,128)(2,1)S(1)}, bf16[48,2048]{1,0:T(8,128)(2,1)S(1)}, u32[]{:S(2)}, u32[]{:S(2)}) %collective-permute-start) | collective-permute-done | bytes 196640 | tf_op jit(solution)/shard_map/while/body/eval_jaxpr/ppermute | solution.py:28
  246.7 5.3 all_gather.28
  252.6 10.4 %conditional.6 = (bf16[48,1024]{1,0:T(8,128)(2,1)S(1)}) conditional(s32[]{:T(128)} %convert_element_type.148, () %tuple.64, (bf16[48,4096]{1,0:T(8,128)(2,1)S(1)}, f32[1,4096]{1,0:T(1,128)S(1)}, bf16[4096,1024]{1,0:T(8,128)(2,1)}, s32[]{:T(128)}, bf16[4096,1024]{1,0:T(8,128)(2,1)}, /*index=5*/bf16[4096,1024]{1,0:T(8,128)(2,1)}) %tuple.65), branch_computations={%region_2.2_spmd, %region_3.5_spmd} | conditional | flops 1220644480 | bytes 78157736 | solution.py:136
  252.9 5.2 fusion.5
  267.2 4.9 conditional.7
  274.5 8.7 %collective-permute-done = bf16[48,2048]{1,0:T(8,128)(2,1)S(1)} collective-permute-done((bf16[48,2048]{1,0:T(8,128)(2,1)S(1)}, bf16[48,2048]{1,0:T(8,128)(2,1)S(1)}, u32[]{:S(2)}, u32[]{:S(2)}) %collective-permute-start) | collective-permute-done | bytes 196640 | tf_op jit(solution)/shard_map/while/body/eval_jaxpr/ppermute | solution.py:28
  284.1 5.2 all_gather.28
  289.9 10.4 %conditional.6 = (bf16[48,1024]{1,0:T(8,128)(2,1)S(1)}) conditional(s32[]{:T(128)} %convert_element_type.148, () %tuple.64, (bf16[48,4096]{1,0:T(8,128)(2,1)S(1)}, f32[1,4096]{1,0:T(1,128)S(1)}, bf16[4096,1024]{1,0:T(8,128)(2,1)}, s32[]{:T(128)}, bf16[4096,1024]{1,0:T(8,128)(2,1)}, /*index=5*/bf16[4096,1024]{1,0:T(8,128)(2,1)}) %tuple.65), branch_computations={%region_2.2_spmd, %region_3.5_spmd} | conditional | flops 1220644480 | bytes 78157736 | solution.py:136
  290.2 5.2 fusion.5
  313.2 7.0 %all_gather.28 = bf16[48,4096]{1,0:T(8,128)(2,1)S(1)} all-gather(bf16[48,2048]{1,0:T(8,128)(2,1)S(1)} %maximum_select_fusion.2), channel_id=1, replica_groups=mesh['section'=4,'tp'=2,'doc'=32] {'tp'}, dimensions={1}, use_global_device_ids=true | all-gather | bytes 589824 | tf_op jit(solution)/shard_map/while/body/eval_jaxpr/all_gather | solution.py:135
  325.0 20.5 %collective-permute-start = (bf16[48,2048]{1,0:T(8,128)(2,1)S(1)}, bf16[48,2048]{1,0:T(8,128)(2,1)S(1)}, u32[]{:S(2)}, u32[]{:S(2)}) collective-permute-start(bf16[48,2048]{1,0:T(8,128)(2,1)S(1)} %add_convert_fusion.2), channel_id=1, source_target_pairs={{192,0},{0,64},{64,128},{128,192},{193,1},{1,65},{65,129},{129,193... | collective-permute-start | bytes 589832 | tf_op jit(solution)/shard_map/while/body/eval_jaxpr/ppermute | solution.py:28
  349.8 5.4 all_gather.28
  360.0 6.7 %collective-permute-start = (bf16[48,2048]{1,0:T(8,128)(2,1)S(1)}, bf16[48,2048]{1,0:T(8,128)(2,1)S(1)}, u32[]{:S(2)}, u32[]{:S(2)}) collective-permute-start(bf16[48,2048]{1,0:T(8,128)(2,1)S(1)} %add_convert_fusion.2), channel_id=1, source_target_pairs={{192,0},{0,64},{64,128},{128,192},{193,1},{1,65},{65,129},{129,193... | collective-permute-start | bytes 589832 | tf_op jit(solution)/shard_map/while/body/eval_jaxpr/ppermute | solution.py:28
  373.5 5.2 all_gather.28
  379.3 10.4 %conditional.6 = (bf16[48,1024]{1,0:T(8,128)(2,1)S(1)}) conditional(s32[]{:T(128)} %convert_element_type.148, () %tuple.64, (bf16[48,4096]{1,0:T(8,128)(2,1)S(1)}, f32[1,4096]{1,0:T(1,128)S(1)}, bf16[4096,1024]{1,0:T(8,128)(2,1)}, s32[]{:T(128)}, bf16[4096,1024]{1,0:T(8,128)(2,1)}, /*index=5*/bf16[4096,1024]{1,0:T(8,128)(2,1)}) %tuple.65), branch_computations={%region_2.2_spmd, %region_3.5_spmd} | conditional | flops 1220644480 | bytes 78157736 | solution.py:136
  379.5 5.2 fusion.5
  401.2 7.8 %collective-permute-done = bf16[48,2048]{1,0:T(8,128)(2,1)S(1)} collective-permute-done((bf16[48,2048]{1,0:T(8,128)(2,1)S(1)}, bf16[48,2048]{1,0:T(8,128)(2,1)S(1)}, u32[]{:S(2)}, u32[]{:S(2)}) %collective-permute-start) | collective-permute-done | bytes 196640 | tf_op jit(solution)/shard_map/while/body/eval_jaxpr/ppermute | solution.py:28
  409.9 5.2 all_gather.28
  415.7 10.4 %conditional.6 = (bf16[48,1024]{1,0:T(8,128)(2,1)S(1)}) conditional(s32[]{:T(128)} %convert_element_type.148, () %tuple.64, (bf16[48,4096]{1,0:T(8,128)(2,1)S(1)}, f32[1,4096]{1,0:T(1,128)S(1)}, bf16[4096,1024]{1,0:T(8,128)(2,1)}, s32[]{:T(128)}, bf16[4096,1024]{1,0:T(8,128)(2,1)}, /*index=5*/bf16[4096,1024]{1,0:T(8,128)(2,1)}) %tuple.65), branch_computations={%region_2.2_spmd, %region_3.5_spmd} | conditional | flops 1220644480 | bytes 78157736 | solution.py:136
  415.9 5.2 fusion.5
  439.0 7.0 %all_gather.28 = bf16[48,4096]{1,0:T(8,128)(2,1)S(1)} all-gather(bf16[48,2048]{1,0:T(8,128)(2,1)S(1)} %maximum_select_fusion.2), channel_id=1, replica_groups=mesh['section'=4,'tp'=2,'doc'=32] {'tp'}, dimensions={1}, use_global_device_ids=true | all-gather | bytes 589824 | tf_op jit(solution)/shard_map/while/body/eval_jaxpr/all_gather | solution.py:135
  450.8 20.1 %collective-permute-start = (bf16[48,2048]{1,0:T(8,128)(2,1)S(1)}, bf16[48,2048]{1,0:T(8,128)(2,1)S(1)}, u32[]{:S(2)}, u32[]{:S(2)}) collective-permute-start(bf16[48,2048]{1,0:T(8,128)(2,1)S(1)} %add_convert_fusion.2), channel_id=1, source_target_pairs={{192,0},{0,64},{64,128},{128,192},{193,1},{1,65},{65,129},{129,193... | collective-permute-start | bytes 589832 | tf_op jit(solution)/shard_map/while/body/eval_jaxpr/ppermute | solution.py:28
  475.2 6.5 %all_gather.28 = bf16[48,4096]{1,0:T(8,128)(2,1)S(1)} all-gather(bf16[48,2048]{1,0:T(8,128)(2,1)S(1)} %maximum_select_fusion.2), channel_id=1, replica_groups=mesh['section'=4,'tp'=2,'doc'=32] {'tp'}, dimensions={1}, use_global_device_ids=true | all-gather | bytes 589824 | tf_op jit(solution)/shard_map/while/body/eval_jaxpr/all_gather | solution.py:135
  486.5 5.6 %collective-permute-start = (bf16[48,2048]{1,0:T(8,128)(2,1)S(1)}, bf16[48,2048]{1,0:T(8,128)(2,1)S(1)}, u32[]{:S(2)}, u32[]{:S(2)}) collective-permute-start(bf16[48,2048]{1,0:T(8,128)(2,1)S(1)} %add_convert_fusion.2), channel_id=1, source_target_pairs={{192,0},{0,64},{64,128},{128,192},{193,1},{1,65},{65,129},{129,193... | collective-permute-start | bytes 589832 | tf_op jit(solution)/shard_map/while/body/eval_jaxpr/ppermute | solution.py:28
  494.7 17.5 %psum.15 = f32[2,2048]{1,0:T(2,128)S(1)} all-reduce(f32[2,2048]{1,0:T(2,128)S(1)} %get-tuple-element.366), channel_id=1, replica_groups=mesh['section'=4,'tp'=2,'doc'=32] {'section'}, use_global_device_ids=true, to_apply=%region_10.11 | all-reduce | flops 4096 | bytes 32768 | tf_op jit(solution)/shard_map/psum | solution.py:165
  512.4 17.9 %all_to_all.5 = f32[32,2,2048]{2,1,0:T(2,128)S(1)} all-to-all(f32[32,2,2048]{2,1,0:T(2,128)S(1)} %broadcast_in_dim.106), channel_id=1, replica_groups=mesh['section'=4,'tp'=2,'doc'=32] {'doc'}, dimensions={0} | all-to-all | bytes 1048576 | tf_op jit(solution)/shard_map/all_to_all | solution.py:39
  (237 shorter events, 129.0 us)
Async XLA Ops:
  7.4 190.0 %all-gather.2.cloned.1.call-start = ((), (), s32[]{:S(2)}) async-start(), calls=%async_computation.2 | async-start | bytes 25952256 | tf_op jit(solution)/shard_map/all_gather | solution.py:21
  9.5 204.8 %all-reduce.2.cloned.1.call-start = ((), (), s32[]{:S(2)}) async-start(), calls=%async_computation.1 | async-start | bytes 1048576 | tf_op jit(solution)/shard_map/psum | solution.py:112
  21.7 192.6 %copy-start = (f32[1,4096]{1,0:T(1,128)S(1)}, f32[1,4096]{1,0:T(1,128)}, u32[]{:S(2)}) copy-start(f32[1,4096]{1,0:T(1,128)} %param.20) | copy-start | bytes 49156
  21.7 192.6 %copy-start.1 = (bf16[16,2048]{1,0:T(8,128)(2,1)S(1)}, bf16[16,2048]{1,0:T(8,128)(2,1)}, u32[]{:S(2)}) copy-start(bf16[16,2048]{1,0:T(8,128)(2,1)} %param.19) | copy-start | bytes 196612
  21.8 192.6 %copy-start.2 = (s32[2,2]{1,0:T(2,128)S(1)}, s32[2,2]{1,0:T(2,128)}, u32[]{:S(2)}) copy-start(s32[2,2]{1,0:T(2,128)} %param.17) | copy-start | bytes 52
  226.0 19.8 %collective-permute-start = (bf16[48,2048]{1,0:T(8,128)(2,1)S(1)}, bf16[48,2048]{1,0:T(8,128)(2,1)S(1)}, u32[]{:S(2)}, u32[]{:S(2)}) collective-permute-start(bf16[48,2048]{1,0:T(8,128)(2,1)S(1)} %add_convert_fusion.2), channel_id=1, source_target_pairs={{192,0},{0,64},{64,128},{128,192},{193,1},{1,65},{65,129},{129,193... | collective-permute-start | bytes 589832 | tf_op jit(solution)/shard_map/while/body/eval_jaxpr/ppermute | solution.py:28
  252.6 5.4 slice-start
  252.8 5.7 %slice-start.1 = ((s8[8388608]{0:T(1024)(128)(4,1)}), s8[4194304]{0:T(1024)(128)(4,1)S(1)}, s32[]{:S(2)}) async-start(s8[8388608]{0:T(1024)(128)(4,1)} %bitcast.43), calls=%async_computation.4 | async-start | bytes 8388608 | tf_op jit(solution)/shard_map/while/body/eval_jaxpr/cond
  252.8 8.3 %slice-start.2 = ((s8[8388608]{0:T(1024)(128)(4,1)}), s8[4194304]{0:T(1024)(128)(4,1)S(1)}, s32[]{:S(2)}) async-start(s8[8388608]{0:T(1024)(128)(4,1)} %bitcast.45), calls=%async_computation.5 | async-start | bytes 8388608 | tf_op jit(solution)/shard_map/while/body/eval_jaxpr/cond
  258.5 2.6 slice-start.3
  272.2 10.9 %collective-permute-start = (bf16[48,2048]{1,0:T(8,128)(2,1)S(1)}, bf16[48,2048]{1,0:T(8,128)(2,1)S(1)}, u32[]{:S(2)}, u32[]{:S(2)}) collective-permute-start(bf16[48,2048]{1,0:T(8,128)(2,1)S(1)} %add_convert_fusion.2), channel_id=1, source_target_pairs={{192,0},{0,64},{64,128},{128,192},{193,1},{1,65},{65,129},{129,193... | collective-permute-start | bytes 589832 | tf_op jit(solution)/shard_map/while/body/eval_jaxpr/ppermute | solution.py:28
  289.9 5.4 slice-start
  290.1 5.7 %slice-start.1 = ((s8[8388608]{0:T(1024)(128)(4,1)}), s8[4194304]{0:T(1024)(128)(4,1)S(1)}, s32[]{:S(2)}) async-start(s8[8388608]{0:T(1024)(128)(4,1)} %bitcast.43), calls=%async_computation.4 | async-start | bytes 8388608 | tf_op jit(solution)/shard_map/while/body/eval_jaxpr/cond
  290.1 8.3 %slice-start.2 = ((s8[8388608]{0:T(1024)(128)(4,1)}), s8[4194304]{0:T(1024)(128)(4,1)S(1)}, s32[]{:S(2)}) async-start(s8[8388608]{0:T(1024)(128)(4,1)} %bitcast.45), calls=%async_computation.5 | async-start | bytes 8388608 | tf_op jit(solution)/shard_map/while/body/eval_jaxpr/cond
  295.8 2.6 slice-start.3
  309.5 2.7 collective-permute-start
  325.0 23.7 %collective-permute-start = (bf16[48,2048]{1,0:T(8,128)(2,1)S(1)}, bf16[48,2048]{1,0:T(8,128)(2,1)S(1)}, u32[]{:S(2)}, u32[]{:S(2)}) collective-permute-start(bf16[48,2048]{1,0:T(8,128)(2,1)S(1)} %add_convert_fusion.2), channel_id=1, source_target_pairs={{192,0},{0,64},{64,128},{128,192},{193,1},{1,65},{65,129},{129,193... | collective-permute-start | bytes 589832 | tf_op jit(solution)/shard_map/while/body/eval_jaxpr/ppermute | solution.py:28
  360.0 12.5 %collective-permute-start = (bf16[48,2048]{1,0:T(8,128)(2,1)S(1)}, bf16[48,2048]{1,0:T(8,128)(2,1)S(1)}, u32[]{:S(2)}, u32[]{:S(2)}) collective-permute-start(bf16[48,2048]{1,0:T(8,128)(2,1)S(1)} %add_convert_fusion.2), channel_id=1, source_target_pairs={{192,0},{0,64},{64,128},{128,192},{193,1},{1,65},{65,129},{129,193... | collective-permute-start | bytes 589832 | tf_op jit(solution)/shard_map/while/body/eval_jaxpr/ppermute | solution.py:28
  379.3 5.4 slice-start
  379.5 5.7 %slice-start.1 = ((s8[8388608]{0:T(1024)(128)(4,1)}), s8[4194304]{0:T(1024)(128)(4,1)S(1)}, s32[]{:S(2)}) async-start(s8[8388608]{0:T(1024)(128)(4,1)} %bitcast.43), calls=%async_computation.4 | async-start | bytes 8388608 | tf_op jit(solution)/shard_map/while/body/eval_jaxpr/cond
  379.5 8.3 %slice-start.2 = ((s8[8388608]{0:T(1024)(128)(4,1)}), s8[4194304]{0:T(1024)(128)(4,1)S(1)}, s32[]{:S(2)}) async-start(s8[8388608]{0:T(1024)(128)(4,1)} %bitcast.45), calls=%async_computation.5 | async-start | bytes 8388608 | tf_op jit(solution)/shard_map/while/body/eval_jaxpr/cond
  385.2 2.6 slice-start.3
  398.9 10.0 %collective-permute-start = (bf16[48,2048]{1,0:T(8,128)(2,1)S(1)}, bf16[48,2048]{1,0:T(8,128)(2,1)S(1)}, u32[]{:S(2)}, u32[]{:S(2)}) collective-permute-start(bf16[48,2048]{1,0:T(8,128)(2,1)S(1)} %add_convert_fusion.2), channel_id=1, source_target_pairs={{192,0},{0,64},{64,128},{128,192},{193,1},{1,65},{65,129},{129,193... | collective-permute-start | bytes 589832 | tf_op jit(solution)/shard_map/while/body/eval_jaxpr/ppermute | solution.py:28
  415.7 5.4 slice-start
  415.9 5.7 %slice-start.1 = ((s8[8388608]{0:T(1024)(128)(4,1)}), s8[4194304]{0:T(1024)(128)(4,1)S(1)}, s32[]{:S(2)}) async-start(s8[8388608]{0:T(1024)(128)(4,1)} %bitcast.43), calls=%async_computation.4 | async-start | bytes 8388608 | tf_op jit(solution)/shard_map/while/body/eval_jaxpr/cond
  415.9 8.3 %slice-start.2 = ((s8[8388608]{0:T(1024)(128)(4,1)}), s8[4194304]{0:T(1024)(128)(4,1)S(1)}, s32[]{:S(2)}) async-start(s8[8388608]{0:T(1024)(128)(4,1)} %bitcast.45), calls=%async_computation.5 | async-start | bytes 8388608 | tf_op jit(solution)/shard_map/while/body/eval_jaxpr/cond
  421.6 2.6 slice-start.3
  435.3 2.7 collective-permute-start
  450.8 23.4 %collective-permute-start = (bf16[48,2048]{1,0:T(8,128)(2,1)S(1)}, bf16[48,2048]{1,0:T(8,128)(2,1)S(1)}, u32[]{:S(2)}, u32[]{:S(2)}) collective-permute-start(bf16[48,2048]{1,0:T(8,128)(2,1)S(1)} %add_convert_fusion.2), channel_id=1, source_target_pairs={{192,0},{0,64},{64,128},{128,192},{193,1},{1,65},{65,129},{129,193... | collective-permute-start | bytes 589832 | tf_op jit(solution)/shard_map/while/body/eval_jaxpr/ppermute | solution.py:28
  486.5 8.2 %collective-permute-start = (bf16[48,2048]{1,0:T(8,128)(2,1)S(1)}, bf16[48,2048]{1,0:T(8,128)(2,1)S(1)}, u32[]{:S(2)}, u32[]{:S(2)}) collective-permute-start(bf16[48,2048]{1,0:T(8,128)(2,1)S(1)} %add_convert_fusion.2), channel_id=1, source_target_pairs={{192,0},{0,64},{64,128},{128,192},{193,1},{1,65},{65,129},{129,193... | collective-permute-start | bytes 589832 | tf_op jit(solution)/shard_map/while/body/eval_jaxpr/ppermute | solution.py:28
Sparse Core Ops, SparseCore 0:
  10.7 186.5 all-gather.1
Sparse Core Ops, SparseCore 1:
  21.8 51.6 all-reduce.1
where the time goes:
time: 545 us; the launch traced here: 539 us
  waiting for transfers between devices  211 us (39%)
  blocking collectives  125 us (23%)
  starting transfers between devices  59.3 us (11%)
  matrix products  55.3 us (10%)
  local copies, waits for them, and re-layouts  44.1 us (8%)
  other arithmetic  16.8 us (3%)
  between operations  14.9 us (3%)
  loops' own time  12.8 us (2%)
    all_gather x1, waiting for transfers between devices, side_by_side(): out = lax.all_gather(both, axis, axis=dim, tiled=True)  176 us
    ppermute x9, starting transfers between devices, from_behind(): return lax.ppermute(block, axis, route)  59.2 us
    all_gather x9, blocking collectives, turn(): features = lax.all_gather(hidden, 'tp', axis=1, tiled=True)  52.4 us
    all_gather x9, blocking collectives, turn(): every_head = lax.all_gather(heads_out, 'tp', axis=1, tiled=True)  37.2 us
    ppermute x9, waiting for transfers between devices, from_behind(): return lax.ppermute(block, axis, route)  35.2 us
    dot_general x4, matrix products, attend(): jnp.dot(normed, query_proj, preferred_element_type=jnp.float32)  20.6 us
    dot_general x4, matrix products, turn(): jnp.dot(every_head, out_proj, preferred_element_type=jnp.float32)  19.8 us
    all_to_all x1, blocking collectives, copy_for_each(): return lax.all_to_all(copies, axis, split_axis=0, concat_axis=0, tiled=True)  17.9 us
  transfers between devices with their start and end apart: 11, of which 10 were waited for; matrix products, arithmetic and copies ran while one was open for 7% of the time, Pallas kernels for 0%

commit v1 on v0

v1 whole, which is shorter than its diff:
```python
import math

import jax
import jax.numpy as jnp
from jax import lax
from jax.experimental import pallas as pl
from jax.experimental.pallas import tpu as pltpu
from jax.sharding import PartitionSpec as P

HD = 128
M = 16
L = 32
SEGS = 2
ROWS = M + L
EPSILON = 1e-05
NEGATIVE = -1e30

NY = 4
NZ = 8
KEEP = 80
BOTH = 48
WAVES = 2
NSEC = 4


def kernel(
    tok_ref,
    mem_ref,
    gain_ref,
    len_ref,
    mix_ref,
    wq_ref,
    wk_ref,
    wv_ref,
    wo_ref,
    out_ref,
    weights,
    w_out,
    blocks,
    scaled,
    qkv,
    mixed,
    heads,
    result,
    parts,
    lens,
    lens_in,
    pool_row,
    pool,
    pool_in,
    total,
    cast,
    local_sem,
    y_send,
    y_recv,
    z_send,
    z_recv,
    f_send,
    f_recv,
    len_sem,
    part_send,
    part_recv,
    tok_send,
    tok_recv,
    x_send,
    x_recv,
    a_send,
    a_recv,
    pool_send,
    pool_recv,
    total_send,
    total_recv,
    cast_send,
    cast_recv,
    go_sem,
):
    sec = lax.axis_index("section")
    tp = lax.axis_index("tp")
    doc = lax.axis_index("doc")
    z = doc // NY
    y = doc % NY
    bit = y % 2
    y_mate = y + 1 - 2 * bit
    y_twin = NY - 1 - y
    y_far = NY - 1 - y_mate
    kind = ((y + 1) // 2) % 2
    width = blocks.shape[-1]
    per = w_out.shape[0] // 4
    depth = wq_ref.shape[0]
    slab = NY * depth
    pair = 2 * depth

    def where(section, t, d):
        return {"section": section, "tp": t, "doc": d}

    def remote(src, dst, send, recv, to):
        return pltpu.make_async_remote_copy(
            src_ref=src,
            dst_ref=dst,
            send_sem=send,
            recv_sem=recv,
            device_id=to,
            device_id_type=pl.DeviceIdType.MESH,
        )

    def at_y(other):
        return where(sec, tp, z * NY + other)

    def kind_of(other):
        return ((other + 1) // 2) % 2

    def column(which, other):
        start = pl.multiple_of(kind_of(other) * per, per)
        return pl.ds(start, per)

    sources = (wq_ref, wk_ref, wv_ref)
    own_row = pl.multiple_of(doc * depth, depth)
    both_from = (1 - bit) * KEEP

    own_copies = [
        pltpu.make_async_copy(
            ref.at[:, column(j, y)],
            weights.at[pl.ds(own_row, depth), pl.ds(j * per, per)],
            local_sem.at[j],
        )
        for j, ref in enumerate(sources)
    ]
    wo_copy = pltpu.make_async_copy(wo_ref, w_out, local_sem.at[3])

    def y_copy(n, j, other):
        ref = sources[j]
        if n == 0:
            src = ref.at[:, column(j, other)]
            dst = weights.at[pl.ds(own_row, depth), pl.ds(j * per, per)]
        else:
            first = pl.multiple_of(both_from, 16)
            src = ref.at[pl.ds(first, BOTH), column(j, other)]
            dst = weights.at[
                pl.ds(pl.multiple_of(own_row + both_from, 16), BOTH), pl.ds(j * per, per)
            ]
        return remote(src, dst, y_send.at[n, j], y_recv.at[n, j], at_y(other))

    y_copies = [
        y_copy(n, j, other) for n, other in enumerate((y_mate, y_twin, y_far)) for j in range(3)
    ]

    def rows_a(zz):
        return pl.ds(pl.multiple_of(zz * slab + (y // 2) * pair, pair), pair)

    def rows_b(zz):
        return pl.ds(
            pl.multiple_of(zz * slab + (1 - y // 2) * pair + KEEP, 16), 2 * BOTH
        )

    def chunk_of(way, step):
        return (z + NZ - step) % NZ if way == 0 else (z + step) % NZ

    def z_copy(way, step, part):
        zz = chunk_of(way, step)
        ref = weights.at[rows_a(zz) if part == 0 else rows_b(zz)]
        to = (z + 1) % NZ if way == 0 else (z + NZ - 1) % NZ
        return remote(
            ref,
            ref,
            z_send.at[way, step, part],
            z_recv.at[way, step, part],
            where(sec, tp, to * NY + y),
        )

    def z_sent(way, step, part):
        return step < 3 or (step == 3 and part == way)

    def z_arrival(way, step, part):
        zz = chunk_of(way, step + 1)
        ref = weights.at[rows_a(zz) if part == 0 else rows_b(zz)]
        return remote(
            ref,
            ref,
            z_send.at[way, step, part],
            z_recv.at[way, step, part],
            where(sec, tp, z * NY + y_twin),
        )

    def f_copies(slot, zz):
        base = zz * slab + (y // 2) * pair
        out = []
        for h, start in enumerate((base, base + pair - KEEP)):
            ref = weights.at[pl.ds(pl.multiple_of(start, 16), KEEP)]
            out.append(
                remote(ref, ref, f_send.at[slot, h], f_recv.at[slot, h], at_y(y_twin))
            )
        return out

    slot = tp * 2 + bit
    peers = [
        (tp, y_mate, tp * 2 + 1 - bit),
        (1 - tp, y, (1 - tp) * 2 + bit),
        (1 - tp, y_mate, (1 - tp) * 2 + 1 - bit),
    ]
    everyone = [(tp, y, slot)] + peers

    def first_copy(n, w):
        t, other, _ = peers[n]
        ref = blocks.at[w, tp, bit]
        return remote(
            ref, ref, tok_send.at[0, w, n], x_recv.at[w, slot], where(sec, t, z * NY + other)
        )

    def token_copy(n, w):
        t, other, _ = peers[n]
        ref = blocks.at[WAVES + w, tp, bit, pl.ds(M, L)]
        return remote(
            ref, ref, tok_send.at[1, w, n], tok_recv.at[w, slot], where(sec, t, z * NY + other)
        )

    def part_copy(s):
        index = jnp.maximum(sec - 1, 0)
        return remote(
            tok_ref.at[s], parts.at[index, s], part_send.at[s], part_recv.at[index, s], where(0, tp, doc)
        )

    len_copy = remote(lens, lens_in, len_sem.at[0], len_sem.at[1], at_y(y_mate))

    wo_copy.start()
    for copy in own_copies:
        copy.start()
    for copy in y_copies:
        copy.start()

    @pl.when(sec > 0)
    def _():
        for s in range(SEGS):
            part_copy(s).start()

    lane = lax.broadcasted_iota(jnp.int32, (1, 128), 1)
    mine = (lane >= bit * ROWS) & (lane < bit * ROWS + ROWS)
    for t in range(SEGS * WAVES):
        lens[t : t + 1, :] = jnp.where(mine, len_ref[t % WAVES, t // WAVES], 0)
    for t in range(SEGS * WAVES, 8):
        lens[t : t + 1, :] = jnp.zeros((1, 128), jnp.int32)
    len_copy.start()

    for copy in own_copies:
        copy.wait()
    for n in range(3):
        for j in range(3):
            y_copies[n * 3 + j].wait_recv()

    @pl.when(sec % 2 == 1)
    def _():
        pl.semaphore_wait(go_sem, 1)

    for part in range(2):
        for way in range(2):
            z_copy(way, 0, part).start()
    for copy in f_copies(0, z):
        copy.start()

    @pl.when(sec == 0)
    def _():
        for s in range(SEGS):
            for index in range(NSEC - 1):
                remote(
                    tok_ref.at[s],
                    parts.at[index, s],
                    part_send.at[s],
                    part_recv.at[index, s],
                    where(1, tp, doc),
                ).wait_recv()
            own = pltpu.make_async_copy(tok_ref.at[s], parts.at[NSEC - 1, s], local_sem.at[4 + s])
            own.start()
            own.wait()
            for w in range(WAVES):
                rows = parts[0, s, w] + parts[1, s, w] + parts[2, s, w] + parts[3, s, w]
                blocks[s * WAVES + w, tp, bit, M:, :] = rows
                if s == 0:
                    blocks[w, tp, bit, :M, :] = mem_ref[...]
            for w in range(WAVES):
                for n in range(3):
                    (first_copy if s == 0 else token_copy)(n, w).start()

    for step in range(4):
        for part in range(2):
            for way in range(2):
                if z_sent(way, step, part):
                    z_arrival(way, step, part).wait_recv()
                    if z_sent(way, step + 1, part) and step < 3:
                        z_copy(way, step + 1, part).start()
                    if part == 0:
                        for copy in f_copies(1 + step + 4 * way, chunk_of(way, step + 1)):
                            copy.start()

    for step in range(4):
        for part in range(2):
            for way in range(2):
                if z_sent(way, step, part):
                    z_copy(way, step, part).wait_send()

    @pl.when(sec % 2 == 0)
    def _():
        pl.semaphore_signal(
            go_sem, inc=1, device_id=where(sec + 1, tp, doc), device_id_type=pl.DeviceIdType.MESH
        )

    for k in range(8):
        for copy in f_copies(k, z):
            copy.wait()
    for copy in y_copies:
        copy.wait_send()
    wo_copy.wait()
    len_copy.wait()

    def b_copy(t, n):
        to_tp, other, _ = everyone[n]
        ref = result.at[t]
        dst = blocks.at[t, tp, bit]
        return remote(
            ref, dst, x_send.at[t, n], x_recv.at[t, slot], where((sec + 1) % NSEC, to_tp, z * NY + other)
        )

    def m_copy(t, n):
        to_tp, other, _ = everyone[n]
        return remote(
            result.at[t, pl.ds(0, M)],
            blocks.at[t + WAVES, tp, bit, pl.ds(0, M)],
            x_send.at[t, n],
            x_recv.at[t + WAVES, slot],
            where(0, to_tp, z * NY + other),
        )

    def arrival(t, source, rows, sem):
        ref = blocks.at[t, source // 2, source % 2, rows]
        return remote(ref, ref, x_send.at[0, 0], sem, at_y(y_mate))

    head_slot = tp * 2 + kind
    a_peers = [
        (1 - tp, y, bit, (1 - tp) * 2 + kind),
        (tp, y_mate, 1 - bit, tp * 2 + 1 - kind),
        (1 - tp, y_mate, 1 - bit, (1 - tp) * 2 + 1 - kind),
    ]

    def a_copy(t, n):
        to_tp, other, which, _ = a_peers[n]
        return remote(
            mixed.at[t, which],
            heads.at[t, head_slot],
            a_send.at[t, n],
            a_recv.at[t, head_slot],
            where(sec, to_tp, z * NY + other),
        )

    def a_arrival(t, n):
        source = a_peers[n][3]
        return remote(
            mixed.at[t, 0], heads.at[t, source], a_send.at[t, n], a_recv.at[t, source], at_y(y_mate)
        )

    def pool_copy(w):
        index = jnp.minimum(sec, NSEC - 2)
        return remote(
            pool.at[w], pool_in.at[index, w], pool_send.at[w], pool_recv.at[index, w], where(NSEC - 1, tp, doc)
        )

    def total_copy(w, to):
        return remote(
            total.at[w], cast, total_send.at[w, to // 2], total_recv, where(to, tp, doc)
        )

    all_rows = pl.ds(0, ROWS)
    scale = 1.0 / math.sqrt(HD)

    def task(t, carry):
        s = t // WAVES
        w = t % WAVES

        @pl.when((sec > 0))
        def _():
            for _, _, source in everyone:
                arrival(t, source, all_rows, x_recv.at[t, source]).wait_recv()

        @pl.when((sec == 0) & (s == 0))
        def _():
            for _, _, source in peers:
                arrival(t, source, all_rows, x_recv.at[t, source]).wait_recv()

        @pl.when((sec == 0) & (s == 1))
        def _():
            for _, _, source in peers:
                arrival(t, source, pl.ds(M, L), tok_recv.at[w, source]).wait_recv()
            for _, _, source in everyone:
                arrival(t, source, pl.ds(0, M), x_recv.at[t, source]).wait_recv()

        step = 256
        square = jnp.zeros((2 * ROWS, step), jnp.float32)
        for half in range(2):
            for c in range(0, width, step):
                x = blocks[t, half, :, :, c : c + step].reshape(2 * ROWS, step).astype(jnp.float32)
                square = square + x * x
                k = half * width + c
                scaled[:, k : k + step] = (x * gain_ref[:, k : k + step]).astype(jnp.bfloat16)
        mean_square = jnp.sum(square, -1, keepdims=True) * (1.0 / (2 * width))
        inverse = lax.rsqrt(mean_square + EPSILON)

        def project(j, carry):
            cols = pl.ds(pl.multiple_of(j * per, per), per)
            out = jnp.dot(scaled[...], weights[:, cols], preferred_element_type=jnp.float32)
            qkv[j] = (out * inverse).astype(jnp.bfloat16)
            return carry

        lax.fori_loop(0, 3, project, 0)

        lengths = (lens[pl.ds(t, 1), :] + lens_in[pl.ds(t, 1), :])[:, : 2 * ROWS]
        shape = (2 * ROWS, 2 * ROWS)
        row = lax.broadcasted_iota(jnp.int32, shape, 0)
        col = lax.broadcasted_iota(jnp.int32, shape, 1)
        row_doc = (row >= ROWS).astype(jnp.int32)
        col_doc = (col >= ROWS).astype(jnp.int32)
        i = row - ROWS * row_doc
        j = col - ROWS * col_doc
        allowed = (
            (row_doc == col_doc)
            & ((j < M) | (j - M < lengths))
            & ((j < M) | (i < M) | (j <= i))
        )
        for h in range(per // HD):
            cols = slice(h * HD, (h + 1) * HD)
            scores = (
                lax.dot_general(
                    qkv[0, :, cols],
                    qkv[1, :, cols],
                    (((1,), (1,)), ((), ())),
                    preferred_element_type=jnp.float32,
                )
                * scale
            )
            scores = jnp.where(allowed, scores, NEGATIVE)
            exps = jnp.where(allowed, jnp.exp(scores), 0.0)
            probs = (exps / jnp.sum(exps, -1, keepdims=True)).astype(jnp.bfloat16)
            out = jnp.dot(probs, qkv[2, :, cols], preferred_element_type=jnp.float32)
            mixed[t, :, :, cols] = out.astype(jnp.bfloat16).reshape(2, ROWS, HD)

        for n in range(3):
            a_copy(t, n).start()
        heads[t, head_slot] = mixed[t, bit]
        for n in range(3):
            a_arrival(t, n).wait_recv()

        length = len_ref[w, s]
        position = lax.broadcasted_iota(jnp.int32, (ROWS, 1), 0)
        token_ok = (position >= M) & (position - M < length)
        factor = mix_ref[0] / length.astype(jnp.float32)

        def finish(j, carry):
            cols = pl.ds(pl.multiple_of(j * 512, 512), 512)
            every = jnp.concatenate([heads[t, q] for q in range(4)], axis=1)
            update = jnp.dot(every, w_out[:, cols], preferred_element_type=jnp.float32)
            out = (blocks[t, tp, bit, :, cols].astype(jnp.float32) + update).astype(jnp.bfloat16)
            result[t, :, cols] = out
            summed = jnp.sum(jnp.where(token_ok, out.astype(jnp.float32), 0.0), 0, keepdims=True)
            pool_row[:, cols] = summed * factor
            return carry

        lax.fori_loop(0, width // 512, finish, 0)

        @pl.when(sec < NSEC - 1)
        def _():
            for n in range(4):
                b_copy(t, n).start()

        @pl.when((sec == NSEC - 1) & (s == 0))
        def _():
            for n in range(4):
                m_copy(t, n).start()

        @pl.when(s == 1)
        def _():
            for k in range(width // 128):
                pool[w, k : k + 1, :] = pool_row[:, k * 128 : (k + 1) * 128]

            @pl.when(sec < NSEC - 1)
            def _():
                pool_copy(w).start()

            @pl.when(sec == NSEC - 1)
            def _():
                for index in range(NSEC - 1):
                    remote(
                        pool.at[w],
                        pool_in.at[index, w],
                        pool_send.at[w],
                        pool_recv.at[index, w],
                        where(0, tp, doc),
                    ).wait_recv()
                summed = pool[w] + pool_in[0, w] + pool_in[1, w] + pool_in[2, w]
                total[w] = summed

                @pl.when(w == 0)
                def _():
                    total_copy(0, 0).start()
                    total_copy(0, 2).start()

                @pl.when(w == 1)
                def _():
                    total_copy(1, 1).start()
                    cast[...] = summed

        return carry

    lax.fori_loop(0, SEGS * WAVES, task, 0)

    core = sec % 2
    base = sec - core
    n_docs = NY * NZ

    @pl.when(sec < NSEC - 1)
    def _():
        remote(
            total.at[0], cast, total_send.at[0, 0], total_recv, where(NSEC - 1, tp, doc)
        ).wait_recv()

    def cast_copy(k, which):
        to = base + core if which == 0 else base + 1 - core
        return remote(
            cast,
            out_ref.at[2 * doc + core],
            cast_send.at[which, k],
            cast_recv.at[core, doc],
            where(to, tp, (doc + k) % n_docs),
        )

    cast_copy(0, 1).start()

    def send_row(k, carry):
        cast_copy(k, 0).start()
        cast_copy(k, 1).start()
        return carry

    lax.fori_loop(1, n_docs, send_row, 0)
    out_ref[2 * doc + core] = cast[...]

    def row_arrival(c, d):
        return remote(
            cast, out_ref.at[2 * d + c], cast_send.at[0, 0], cast_recv.at[c, d], where(base + 1 - core, tp, doc)
        )

    row_arrival(1 - core, doc).wait_recv()

    def take_row(k, carry):
        d = (doc + k) % n_docs
        row_arrival(core, d).wait_recv()
        row_arrival(1 - core, d).wait_recv()
        return carry

    lax.fori_loop(1, n_docs, take_row, 0)

    cast_copy(0, 1).wait_send()

    def sent_row(k, carry):
        cast_copy(k, 0).wait_send()
        cast_copy(k, 1).wait_send()
        return carry

    lax.fori_loop(1, n_docs, sent_row, 0)

    @pl.when(sec > 0)
    def _():
        for s in range(SEGS):
            part_copy(s).wait_send()

    @pl.when(sec == 0)
    def _():
        for w in range(WAVES):
            for n in range(3):
                first_copy(n, w).wait_send()
                token_copy(n, w).wait_send()

    def sent_task(t, carry):
        for n in range(3):
            a_copy(t, n).wait_send()

        @pl.when(sec < NSEC - 1)
        def _():
            for n in range(4):
                b_copy(t, n).wait_send()

        @pl.when((sec == NSEC - 1) & (t < WAVES))
        def _():
            for n in range(4):
                m_copy(t, n).wait_send()

        return carry

    lax.fori_loop(0, SEGS * WAVES, sent_task, 0)

    @pl.when(sec < NSEC - 1)
    def _():
        for w in range(WAVES):
            pool_copy(w).wait_send()

    @pl.when(sec == NSEC - 1)
    def _():
        total_copy(0, 0).wait_send()
        total_copy(0, 2).wait_send()
        total_copy(1, 1).wait_send()


def body(
    token_ids,
    seg_lengths,
    emb_table,
    mem_init,
    norm_gain,
    w_query,
    w_key,
    w_value,
    w_out,
    layer_mix,
):
    doc_local = token_ids.shape[0]
    vocab_rows, width = emb_table.shape
    flat_ids = jnp.transpose(token_ids, (1, 0, 2)).reshape(-1)
    local_ids = flat_ids - lax.axis_index("section") * vocab_rows
    owned = (local_ids >= 0) & (local_ids < vocab_rows)
    picked = jnp.take(emb_table, jnp.clip(local_ids, 0, vocab_rows - 1), axis=0)
    tokens = jnp.where(owned[:, None], picked, jnp.zeros((), picked.dtype))
    tokens = tokens.reshape(SEGS, doc_local, L, width)
    depth, head_cols = w_query.shape[1:]
    per = head_cols // 2
    n_tasks = SEGS * WAVES
    dma = pltpu.SemaphoreType.DMA
    bf16, f32 = jnp.bfloat16, jnp.float32
    any_space = pl.BlockSpec(memory_space=pl.ANY)
    vmem = pl.BlockSpec(memory_space=pltpu.VMEM)
    smem = pl.BlockSpec(memory_space=pltpu.SMEM)
    lanes = width // 128
    rows = pl.pallas_call(
        kernel,
        out_shape=jax.ShapeDtypeStruct((NY * NZ * WAVES, lanes, 128), f32),
        in_specs=[any_space, vmem, vmem, smem, smem, any_space, any_space, any_space, any_space],
        out_specs=vmem,
        scratch_shapes=[
            pltpu.VMEM((2 * width, 3 * per), bf16),
            pltpu.VMEM((2 * head_cols, width), bf16),
            pltpu.VMEM((n_tasks, 2, 2, ROWS, width), bf16),
            pltpu.VMEM((2 * ROWS, 2 * width), bf16),
            pltpu.VMEM((3, 2 * ROWS, per), bf16),
            pltpu.VMEM((n_tasks, 2, ROWS, per), bf16),
            pltpu.VMEM((n_tasks, 4, ROWS, per), bf16),
            pltpu.VMEM((n_tasks, ROWS, width), bf16),
            pltpu.VMEM((NSEC, SEGS, WAVES, L, width), bf16),
            pltpu.VMEM((8, 128), jnp.int32),
            pltpu.VMEM((8, 128), jnp.int32),
            pltpu.VMEM((1, width), f32),
            pltpu.VMEM((WAVES, lanes, 128), f32),
            pltpu.VMEM((NSEC - 1, WAVES, lanes, 128), f32),
            pltpu.VMEM((WAVES, lanes, 128), f32),
            pltpu.VMEM((lanes, 128), f32),
            dma((6,)),
            dma((3, 3)),
            dma((3, 3)),
            dma((2, 4, 2)),
            dma((2, 4, 2)),
            dma((8, 2)),
            dma((8, 2)),
            dma((2,)),
            dma((SEGS,)),
            dma((NSEC - 1, SEGS)),
            dma((SEGS, WAVES, 3)),
            dma((WAVES, 4)),
            dma((n_tasks, 4)),
            dma((n_tasks, 4)),
            dma((n_tasks, 3)),
            dma((n_tasks, 4)),
            dma((WAVES,)),
            dma((NSEC - 1, WAVES)),
            dma((WAVES, 2)),
            dma,
            dma((2, NY * NZ)),
            dma((2, NY * NZ)),
            pltpu.SemaphoreType.REGULAR,
        ],
        compiler_params=pltpu.CompilerParams(
            has_side_effects=True, vmem_limit_bytes=48 * 1024 * 1024
        ),
    )(
        tokens,
        mem_init,
        norm_gain,
        seg_lengths,
        layer_mix,
        w_query[0],
        w_key[0],
        w_value[0],
        w_out[0],
    )
    return rows.reshape(NY * NZ * WAVES, width)


def solution(mesh):
    return jax.shard_map(
        body,
        mesh=mesh,
        in_specs=(
            P("doc", None, None),
            P("doc", None),
            P("section", "tp"),
            P(None, "tp"),
            P("section", None),
            P("section", "doc", "tp"),
            P("section", "doc", "tp"),
            P("section", "doc", "tp"),
            P("section", None, "tp"),
            P("section"),
        ),
        out_specs=P(None, "tp"),
        check_vma=False,
    )
```

time: 545 us -> 298 us (0.55); the launches traced: 539 us -> 297 us
  Pallas kernels: 0 us -> 280 us
  waiting for transfers between devices: 211 us -> 0 us
  blocking collectives: 125 us -> 0 us
  starting transfers between devices: 59.3 us -> 0 us
  matrix products: 55.3 us -> 0 us
  local copies, waits for them, and re-layouts: 44.1 us -> 15.5 us
  other arithmetic: 16.8 us -> 0.86 us
  between operations: 14.9 us -> 0.71 us
  loops' own time: 12.8 us -> 0 us
    pallas_call x0 -> x1, Pallas kernels: none -> 280 us  [body(): pl.pallas_call(kernel, out_shape=jax.ShapeDtypeStruct((NY * NZ * WAVES, l...]
    all_gather x1 -> x0, waiting for transfers between devices: 176 us -> none  [side_by_side(): out = lax.all_gather(both, axis, axis=dim, tiled=True)]
    all_gather x18 -> x0, blocking collectives: 89.6 us -> none  [the longest x9 52.4 us: turn(): features = lax.all_gather(hidden, 'tp', axis=1, tiled=True)]
    ppermute x9 -> x0, starting transfers between devices: 59.2 us -> none  [from_behind(): return lax.ppermute(block, axis, route)]
    dot_general x24 -> x0, matrix products: 55.3 us -> none  [the longest x4 20.6 us: attend(): jnp.dot(normed, query_proj, preferred_element_type=jnp.float32)]
    ppermute x9 -> x0, waiting for transfers between devices: 35.2 us -> none  [from_behind(): return lax.ppermute(block, axis, route)]
    all_to_all x1 -> x0, blocking collectives: 17.9 us -> none  [copy_for_each(): return lax.all_to_all(copies, axis, split_axis=0, concat_axis=0, tiled=True)]
    psum x1 -> x0, blocking collectives: 17.5 us -> none  [body(): layer_total = lax.psum(pooled, 'section')]
  transfers between devices with their start and end apart: 11 -> 0, of which waited for: 10 -> 0; matrix products, arithmetic and copies ran while one was open for 7% -> 0% of each run, Pallas kernels for 0% -> 0%
where the time goes in v1:
time: 298 us; the launch traced here: 297 us
  Pallas kernels  280 us (94%)
  local copies, waits for them, and re-layouts  15.5 us (5%)
    pallas_call x1, Pallas kernels, body(): pl.pallas_call(kernel, out_shape=jax.ShapeDtypeStruct((NY * NZ * WAVES, l...  280 us
    gather x1, local copies, waits for them, and re-layouts, body(): picked = jnp.take(emb_table, jnp.clip(local_ids, 0, vocab_rows - 1), axis=0)  9.37 us
    unnamed x13, local copies, waits for them, and re-layouts  6.03 us

profile of v1, /device:TPU:1, one launch (start us, length us, event | category | flops | bytes accessed | tf_op | source)
XLA Modules:
  0.0 297.4 jit_solution(9513996211413563529)
XLA Ops:
  0.0 0.7 compare_and_fusion
  0.7 0.1 min.15
  0.8 9.4 %gather_fusion = bf16[128,2048]{1,0:T(8,128)(2,1)S(1)} fusion(bf16[4096,2048]{1,0:T(8,128)(2,1)} %param.12, s32[1024]{0:T(1024)S(1)} %pad_clamp_fusion), kind=kCustom, calls=%fused_computation | custom fusion | bytes 1049088 | tf_op jit(solution)/shard_map/jit(_take)/gather | solution.py:624
  10.2 0.1 select_select_fusion.tok_ref
  11.0 0.0 copy-start
  11.0 0.9 copy-done
  12.0 0.0 copy-start.1
  12.0 0.9 copy-done.1
  12.9 0.0 copy-start.2
  12.9 0.9 copy-done.2
  13.9 0.0 copy-start.3
  13.9 0.8 copy-done.3
  14.7 0.0 copy-start.4
  14.7 0.7 copy-done.4
  15.4 0.0 copy-start.5
  15.4 0.7 copy-done.5
  16.1 280.3 %shard_map.100 = f32[64,16,128]{2,1,0:T(8,128)S(1)} custom-call(bf16[2,2,32,2048]{3,2,1,0:T(8,128)(2,1)S(1)} %select_select_fusion.tok_ref, bf16[16,2048]{1,0:T(8,128)(2,1)S(1)} %copy-done.3, f32[1,4096]{1,0:T(1,128)S(1)} %copy-done.4, s32[2,2]{1,0:T(2,128)S(1)} %copy-done.5, f32[1]{0:T(128)S(6)} %copy.21.mix_ref, bf16[128,1024]{1,0:T(8,128)(2,1)S(1)} %bitcast.18, ...), custom_call_target="tpu_custom_call" | custom-call | tf_op jit(solution)/shard_map/pallas_call | solution.py:636
  296.4 1.0 copy.20
  (6 shorter events, 0.0 us)
Async XLA Ops:
  11.0 1.0 copy-start
  12.0 0.9 copy-start.1
  12.9 0.9 copy-start.2
  13.9 0.8 copy-start.3
  14.7 0.7 copy-start.4
  15.4 0.7 copy-start.5

commit v2 on v1

--- a/solution.py
+++ b/solution.py
@@ -24,20 +24,29 @@
 
 
 def kernel(
-    tok_ref,
-    mem_ref,
-    gain_ref,
-    len_ref,
-    mix_ref,
+    ids_hbm,
+    table_hbm,
+    mem_hbm,
+    gain_hbm,
+    len_hbm,
+    mix_hbm,
     wq_ref,
     wk_ref,
     wv_ref,
     wo_ref,
     out_ref,
+    ids_ref,
+    table,
+    picks,
+    mem_ref,
+    gain_ref,
+    len_ref,
+    mix_ref,
     weights,
     w_out,
     blocks,
     scaled,
+    qkv_sum,
     qkv,
     mixed,
     heads,
@@ -64,6 +73,7 @@
     tok_recv,
     x_send,
     x_recv,
+    r_send,
     a_send,
     a_recv,
     pool_send,
@@ -216,21 +226,46 @@
     def part_copy(s):
         index = jnp.maximum(sec - 1, 0)
         return remote(
-            tok_ref.at[s], parts.at[index, s], part_send.at[s], part_recv.at[index, s], where(0, tp, doc)
+            parts.at[NSEC - 1, s], parts.at[index, s], part_send.at[s], part_recv.at[index, s], where(0, tp, doc)
         )
 
     len_copy = remote(lens, lens_in, len_sem.at[0], len_sem.at[1], at_y(y_mate))
 
-    wo_copy.start()
-    for copy in own_copies:
+    small_copies = [
+        pltpu.make_async_copy(len_hbm, len_ref, local_sem.at[4]),
+        pltpu.make_async_copy(mix_hbm, mix_ref, local_sem.at[5]),
+        pltpu.make_async_copy(ids_hbm, ids_ref, local_sem.at[6]),
+        pltpu.make_async_copy(mem_hbm, mem_ref, local_sem.at[7]),
+        pltpu.make_async_copy(gain_hbm.at[:, pl.ds(0, width)], gain_ref.at[0], local_sem.at[8]),
+        pltpu.make_async_copy(gain_hbm.at[:, pl.ds(width, width)], gain_ref.at[1], local_sem.at[9]),
+    ]
+    table_copy = pltpu.make_async_copy(table_hbm, table, local_sem.at[10])
+    for copy in small_copies + own_copies:
         copy.start()
+
+    next_sec = (sec + 1) % NSEC
+    last_sec = (sec + NSEC - 1) % NSEC
+    greeted = [where(sec, tp, z * NY + other) for other in (y_mate, y_twin, y_far)]
+    greeted += [where(sec, 1 - tp, z * NY + other) for other in (y, y_mate)]
+    greeted += [where(sec, tp, (z + step) % NZ * NY + y) for step in (1, NZ - 1)]
+    greeted += [
+        where(to, t, z * NY + other)
+        for to in (next_sec, last_sec)
+        for t in (tp, 1 - tp)
+        for other in (y, y_mate)
+    ]
+    greeted += [where((sec + 2) % NSEC, tp, doc)]
+    barrier = pltpu.get_barrier_semaphore()
+    for to in greeted:
+        pl.semaphore_signal(barrier, inc=1, device_id=to, device_id_type=pl.DeviceIdType.MESH)
+    pl.semaphore_wait(barrier, len(greeted))
+
     for copy in y_copies:
         copy.start()
-
-    @pl.when(sec > 0)
-    def _():
-        for s in range(SEGS):
-            part_copy(s).start()
+    table_copy.start()
+    wo_copy.start()
+    for copy in small_copies:
+        copy.wait()
 
     lane = lax.broadcasted_iota(jnp.int32, (1, 128), 1)
     mine = (lane >= bit * ROWS) & (lane < bit * ROWS + ROWS)
@@ -246,30 +281,61 @@
         for j in range(3):
             y_copies[n * 3 + j].wait_recv()
 
+    def start_z():
+        for part in range(2):
+            for way in range(2):
+                z_copy(way, 0, part).start()
+        for copy in f_copies(0, z):
+            copy.start()
+
+    @pl.when(sec % 2 == 0)
+    def _():
+        start_z()
+
+    n_ids = SEGS * WAVES * L
+    eye = lax.broadcasted_iota(jnp.int32, (L, L), 0) == lax.broadcasted_iota(jnp.int32, (L, L), 1)
+    columns = [
+        jnp.sum(
+            jnp.where(eye, ids_ref[w, s : s + 1, :].astype(jnp.float32), 0.0), -1, keepdims=True
+        )
+        for s in range(SEGS)
+        for w in range(WAVES)
+    ]
+    wanted = jnp.concatenate(columns, axis=0).astype(jnp.int32) - sec * table.shape[0]
+    for k in range(0, table.shape[0], 512):
+        place = lax.broadcasted_iota(jnp.int32, (n_ids, 512), 1) + k
+        picks[:, k : k + 512] = jnp.where(place == wanted, 1.0, 0.0).astype(jnp.bfloat16)
+    table_copy.wait()
+
+    def pick(j, carry):
+        cols = pl.ds(pl.multiple_of(j * 512, 512), 512)
+        rows = jnp.dot(picks[...], table[:, cols], preferred_element_type=jnp.float32)
+        parts[NSEC - 1, :, :, :, cols] = rows.astype(jnp.bfloat16).reshape(SEGS, WAVES, L, 512)
+        return carry
+
+    lax.fori_loop(0, width // 512, pick, 0)
+
+    @pl.when(sec > 0)
+    def _():
+        for s in range(SEGS):
+            part_copy(s).start()
+
     @pl.when(sec % 2 == 1)
     def _():
         pl.semaphore_wait(go_sem, 1)
-
-    for part in range(2):
-        for way in range(2):
-            z_copy(way, 0, part).start()
-    for copy in f_copies(0, z):
-        copy.start()
+        start_z()
 
     @pl.when(sec == 0)
     def _():
         for s in range(SEGS):
             for index in range(NSEC - 1):
                 remote(
-                    tok_ref.at[s],
+                    parts.at[NSEC - 1, s],
                     parts.at[index, s],
                     part_send.at[s],
                     part_recv.at[index, s],
                     where(1, tp, doc),
                 ).wait_recv()
-            own = pltpu.make_async_copy(tok_ref.at[s], parts.at[NSEC - 1, s], local_sem.at[4 + s])
-            own.start()
-            own.wait()
             for w in range(WAVES):
                 rows = parts[0, s, w] + parts[1, s, w] + parts[2, s, w] + parts[3, s, w]
                 blocks[s * WAVES + w, tp, bit, M:, :] = rows
@@ -310,22 +376,43 @@
     wo_copy.wait()
     len_copy.wait()
 
+    near = sec % 2 == 0
+
     def b_copy(t, n):
         to_tp, other, _ = everyone[n]
-        ref = result.at[t]
-        dst = blocks.at[t, tp, bit]
-        return remote(
-            ref, dst, x_send.at[t, n], x_recv.at[t, slot], where((sec + 1) % NSEC, to_tp, z * NY + other)
+        return remote(
+            result.at[t],
+            blocks.at[t, tp, bit],
+            x_send.at[t, n],
+            x_recv.at[t, slot],
+            where((sec + 1) % NSEC, to_tp, z * NY + other),
+        )
+
+    hop = [y, y_mate]
+
+    def h_copy(t, n):
+        return remote(
+            result.at[t],
+            blocks.at[t, tp, bit],
+            x_send.at[t, n],
+            x_recv.at[t, slot],
+            where((sec + 1) % NSEC, 1 - tp, z * NY + hop[n]),
         )
 
     def m_copy(t, n):
-        to_tp, other, _ = everyone[n]
         return remote(
             result.at[t, pl.ds(0, M)],
             blocks.at[t + WAVES, tp, bit, pl.ds(0, M)],
             x_send.at[t, n],
             x_recv.at[t + WAVES, slot],
-            where(0, to_tp, z * NY + other),
+            where(0, 1 - tp, z * NY + hop[n]),
+        )
+
+    def forward(t, n, rows):
+        which = bit if n == 0 else 1 - bit
+        ref = blocks.at[t, 1 - tp, which, rows]
+        return remote(
+            ref, ref, r_send.at[t, n], x_recv.at[t, (1 - tp) * 2 + which], where(sec, 1 - tp, doc)
         )
 
     def arrival(t, source, rows, sem):
@@ -373,41 +460,73 @@
         s = t // WAVES
         w = t % WAVES
 
-        @pl.when((sec > 0))
-        def _():
-            for _, _, source in everyone:
+        step = 256
+        first = jnp.where(near & ((sec > 0) | (s == 1)), 1 - tp, tp)
+
+        def take(half, rows, t):
+            for d in (bit, 1 - bit):
+                source = half * 2 + d
+                arrival(t, source, rows, x_recv.at[t, source]).wait_recv()
+
+        def wait_half(n):
+            half = first if n == 0 else 1 - first
+
+            @pl.when(sec % 2 == 1)
+            def _():
+                take(half, all_rows, t)
+
+            @pl.when(sec == 2)
+            def _():
+                for k, d in enumerate((bit, 1 - bit)):
+                    source = half * 2 + d
+                    arrival(t, source, all_rows, x_recv.at[t, source]).wait_recv()
+                    if n == 0:
+                        forward(t, k, all_rows).start()
+
+            @pl.when((sec == 0) & (s == 0))
+            def _():
+                source = half * 2 + 1 - bit
                 arrival(t, source, all_rows, x_recv.at[t, source]).wait_recv()
-
-        @pl.when((sec == 0) & (s == 0))
-        def _():
-            for _, _, source in peers:
-                arrival(t, source, all_rows, x_recv.at[t, source]).wait_recv()
-
-        @pl.when((sec == 0) & (s == 1))
-        def _():
-            for _, _, source in peers:
+                if n == 1:
+                    source = half * 2 + bit
+                    arrival(t, source, all_rows, x_recv.at[t, source]).wait_recv()
+
+            @pl.when((sec == 0) & (s == 1))
+            def _():
+                source = half * 2 + 1 - bit
                 arrival(t, source, pl.ds(M, L), tok_recv.at[w, source]).wait_recv()
-            for _, _, source in everyone:
-                arrival(t, source, pl.ds(0, M), x_recv.at[t, source]).wait_recv()
-
-        step = 256
+                if n == 0:
+                    source = half * 2 + bit
+                    arrival(t, source, pl.ds(M, L), tok_recv.at[w, source]).wait_recv()
+                for k, d in enumerate((bit, 1 - bit)):
+                    source = half * 2 + d
+                    arrival(t, source, pl.ds(0, M), x_recv.at[t, source]).wait_recv()
+                    if n == 0:
+                        forward(t, k, pl.ds(0, M)).start()
+
         square = jnp.zeros((2 * ROWS, step), jnp.float32)
-        for half in range(2):
+        for n in range(2):
+            half = first if n == 0 else 1 - first
+            wait_half(n)
             for c in range(0, width, step):
                 x = blocks[t, half, :, :, c : c + step].reshape(2 * ROWS, step).astype(jnp.float32)
                 square = square + x * x
-                k = half * width + c
-                scaled[:, k : k + step] = (x * gain_ref[:, k : k + step]).astype(jnp.bfloat16)
-        mean_square = jnp.sum(square, -1, keepdims=True) * (1.0 / (2 * width))
-        inverse = lax.rsqrt(mean_square + EPSILON)
-
-        def project(j, carry):
-            cols = pl.ds(pl.multiple_of(j * per, per), per)
-            out = jnp.dot(scaled[...], weights[:, cols], preferred_element_type=jnp.float32)
-            qkv[j] = (out * inverse).astype(jnp.bfloat16)
-            return carry
-
-        lax.fori_loop(0, 3, project, 0)
+                scaled[:, c : c + step] = (x * gain_ref[half, :, c : c + step]).astype(jnp.bfloat16)
+            if n == 1:
+                mean_square = jnp.sum(square, -1, keepdims=True) * (1.0 / (2 * width))
+                inverse = lax.rsqrt(mean_square + EPSILON)
+            rows = pl.ds(pl.multiple_of(half * width, width), width)
+
+            def project(j, carry):
+                cols = pl.ds(pl.multiple_of(j * per, per), per)
+                out = jnp.dot(scaled[...], weights[rows, cols], preferred_element_type=jnp.float32)
+                if n == 0:
+                    qkv_sum[j] = out
+                else:
+                    qkv[j] = ((qkv_sum[j] + out) * inverse).astype(jnp.bfloat16)
+                return carry
+
+            lax.fori_loop(0, 3, project, 0)
 
         lengths = (lens[pl.ds(t, 1), :] + lens_in[pl.ds(t, 1), :])[:, : 2 * ROWS]
         shape = (2 * ROWS, 2 * ROWS)
@@ -462,14 +581,19 @@
 
         lax.fori_loop(0, width // 512, finish, 0)
 
-        @pl.when(sec < NSEC - 1)
+        @pl.when(near)
         def _():
             for n in range(4):
                 b_copy(t, n).start()
 
+        @pl.when(sec == 1)
+        def _():
+            for n in range(2):
+                h_copy(t, n).start()
+
         @pl.when((sec == NSEC - 1) & (s == 0))
         def _():
-            for n in range(4):
+            for n in range(2):
                 m_copy(t, n).start()
 
         @pl.when(s == 1)
@@ -578,15 +702,30 @@
         for n in range(3):
             a_copy(t, n).wait_send()
 
-        @pl.when(sec < NSEC - 1)
+        @pl.when(near)
         def _():
             for n in range(4):
                 b_copy(t, n).wait_send()
 
+        @pl.when(sec == 1)
+        def _():
+            for n in range(2):
+                h_copy(t, n).wait_send()
+
         @pl.when((sec == NSEC - 1) & (t < WAVES))
         def _():
-            for n in range(4):
+            for n in range(2):
                 m_copy(t, n).wait_send()
+
+        @pl.when(sec == 2)
+        def _():
+            for n in range(2):
+                forward(t, n, all_rows).wait_send()
+
+        @pl.when((sec == 0) & (t >= WAVES))
+        def _():
+            for n in range(2):
+                forward(t, n, pl.ds(0, M)).wait_send()
 
         return carry
 
@@ -618,12 +757,6 @@
 ):
     doc_local = token_ids.shape[0]
     vocab_rows, width = emb_table.shape
-    flat_ids = jnp.transpose(token_ids, (1, 0, 2)).reshape(-1)
-    local_ids = flat_ids - lax.axis_index("section") * vocab_rows
-    owned = (local_ids >= 0) & (local_ids < vocab_rows)
-    picked = jnp.take(emb_table, jnp.clip(local_ids, 0, vocab_rows - 1), axis=0)
-    tokens = jnp.where(owned[:, None], picked, jnp.zeros((), picked.dtype))
-    tokens = tokens.reshape(SEGS, doc_local, L, width)
     depth, head_cols = w_query.shape[1:]
     per = head_cols // 2
     n_tasks = SEGS * WAVES
@@ -631,18 +764,25 @@
     bf16, f32 = jnp.bfloat16, jnp.float32
     any_space = pl.BlockSpec(memory_space=pl.ANY)
     vmem = pl.BlockSpec(memory_space=pltpu.VMEM)
-    smem = pl.BlockSpec(memory_space=pltpu.SMEM)
     lanes = width // 128
     rows = pl.pallas_call(
         kernel,
         out_shape=jax.ShapeDtypeStruct((NY * NZ * WAVES, lanes, 128), f32),
-        in_specs=[any_space, vmem, vmem, smem, smem, any_space, any_space, any_space, any_space],
+        in_specs=[any_space] * 10,
         out_specs=vmem,
         scratch_shapes=[
+            pltpu.VMEM((WAVES, SEGS, L), jnp.int32),
+            pltpu.VMEM((vocab_rows, width), bf16),
+            pltpu.VMEM((n_tasks * L, vocab_rows), bf16),
+            pltpu.VMEM((M, width), bf16),
+            pltpu.VMEM((2, 1, width), f32),
+            pltpu.SMEM((doc_local, SEGS), jnp.int32),
+            pltpu.SMEM((1,), f32),
             pltpu.VMEM((2 * width, 3 * per), bf16),
             pltpu.VMEM((2 * head_cols, width), bf16),
             pltpu.VMEM((n_tasks, 2, 2, ROWS, width), bf16),
-            pltpu.VMEM((2 * ROWS, 2 * width), bf16),
+            pltpu.VMEM((2 * ROWS, width), bf16),
+            pltpu.VMEM((3, 2 * ROWS, per), f32),
             pltpu.VMEM((3, 2 * ROWS, per), bf16),
             pltpu.VMEM((n_tasks, 2, ROWS, per), bf16),
             pltpu.VMEM((n_tasks, 4, ROWS, per), bf16),
@@ -655,7 +795,7 @@
             pltpu.VMEM((NSEC - 1, WAVES, lanes, 128), f32),
             pltpu.VMEM((WAVES, lanes, 128), f32),
             pltpu.VMEM((lanes, 128), f32),
-            dma((6,)),
+            dma((11,)),
             dma((3, 3)),
             dma((3, 3)),
             dma((2, 4, 2)),
@@ -669,6 +809,7 @@
             dma((WAVES, 4)),
             dma((n_tasks, 4)),
             dma((n_tasks, 4)),
+            dma((n_tasks, 2)),
             dma((n_tasks, 3)),
             dma((n_tasks, 4)),
             dma((WAVES,)),
@@ -680,10 +821,11 @@
             pltpu.SemaphoreType.REGULAR,
         ],
         compiler_params=pltpu.CompilerParams(
-            has_side_effects=True, vmem_limit_bytes=48 * 1024 * 1024
+            has_side_effects=True, collective_id=0, vmem_limit_bytes=60 * 1024 * 1024
         ),
     )(
-        tokens,
+        token_ids,
+        emb_table,
         mem_init,
         norm_gain,
         seg_lengths,

time: 298 us -> 286 us (0.960)
  local copies, waits for them, and re-layouts: 15.5 us -> 2 us
  Pallas kernels: 280 us -> 283 us
    gather x1 -> x0, local copies, waits for them, and re-layouts: 9.37 us -> none  [body(): picked = jnp.take(emb_table, jnp.clip(local_ids, 0, vocab_rows - 1), axis=0)]
    unnamed x13 -> x1, local copies, waits for them, and re-layouts: 6.03 us -> 2 us
where the time goes in v2:
time: 286 us; the launch traced here: 285 us
  Pallas kernels  283 us (99%)
    pallas_call x1, Pallas kernels, body(): pl.pallas_call(kernel, out_shape=jax.ShapeDtypeStruct((NY * NZ * WAVES, l...  283 us

profile of v2, /device:TPU:1, one launch (start us, length us, event | category | flops | bytes accessed | tf_op | source)
XLA Modules:
  0.0 285.4 jit_solution(5540678125277462720)
XLA Ops:
  0.7 282.7 %shard_map.100 = f32[64,16,128]{2,1,0:T(8,128)} custom-call(s32[2,2,32]{2,1,0:T(2,128)} %ids_hbm.1, bf16[4096,2048]{1,0:T(8,128)(2,1)} %table_hbm.1, bf16[16,2048]{1,0:T(8,128)(2,1)} %mem_hbm.1, f32[1,4096]{1,0:T(1,128)} %gain_hbm.1, s32[2,2]{1,0:T(2,128)} %len_hbm.1, f32[1]{0:T(128)S(6)} %copy.14.mix_hbm, bf16[128,1024]{1,0:T(8,128)(2,1)} %bitcast.10, ...), custom_call_target="tpu_custom_call" | custom-call | tf_op jit(solution)/shard_map/pallas_call | solution.py:768
  283.4 2.0 copy.13

commit v3 on v2

v3 whole, which is shorter than its diff:
```python
import math

import jax
import jax.numpy as jnp
from jax import lax
from jax.experimental import pallas as pl
from jax.experimental.pallas import tpu as pltpu
from jax.sharding import PartitionSpec as P

HD = 128
M = 16
L = 32
SEGS = 2
ROWS = M + L
EPSILON = 1e-05
NEGATIVE = -1e30

NY = 4
NZ = 8
KEEP = 80
BOTH = 48
WAVES = 2
NSEC = 4


def kernel(
    ids_hbm,
    table_hbm,
    mem_hbm,
    gain_hbm,
    len_hbm,
    mix_hbm,
    wq_ref,
    wk_ref,
    wv_ref,
    wo_ref,
    out_ref,
    ids_ref,
    table,
    picks,
    mem_ref,
    gain_ref,
    len_ref,
    mix_ref,
    weights2,
    weights4,
    w_out,
    blocks,
    scaled,
    sum2,
    sum4,
    qkv2,
    qkv4,
    mixed2,
    mixed4,
    heads,
    result,
    parts,
    lens,
    pool_row,
    pool,
    pool_in,
    total,
    cast,
    local_sem,
    y_send,
    y_recv,
    z_send,
    z_recv,
    f_send,
    f_recv,
    len_send,
    len_recv,
    part_send,
    part_recv,
    tok_send,
    tok_recv,
    x_send,
    x_recv,
    r_send,
    a_send,
    a_recv,
    pool_send,
    pool_recv,
    total_send,
    total_recv,
    cast_send,
    cast_recv,
    go_sem,
):
    sec = lax.axis_index("section")
    tp = lax.axis_index("tp")
    doc = lax.axis_index("doc")
    z = doc // NY
    y = doc % NY
    bit = y % 2
    y_mate = y + 1 - 2 * bit
    y_twin = NY - 1 - y
    y_far = NY - 1 - y_mate
    kind = ((y + 1) // 2) % 2
    width = blocks.shape[-1]
    depth = wq_ref.shape[0]
    slab = NY * depth
    pair = 2 * depth
    heads_cols = wq_ref.shape[1]

    def where(section, t, d):
        return {"section": section, "tp": t, "doc": d}

    def remote(src, dst, send, recv, to):
        return pltpu.make_async_remote_copy(
            src_ref=src,
            dst_ref=dst,
            send_sem=send,
            recv_sem=recv,
            device_id=to,
            device_id_type=pl.DeviceIdType.MESH,
        )

    def at_y(other):
        return where(sec, tp, z * NY + other)

    wide = sec < 2
    ring = [y, y_mate, y_twin, y_far]
    sources = (wq_ref, wk_ref, wv_ref)
    own_row = pl.multiple_of(doc * depth, depth)
    both_from = (1 - bit) * KEEP

    class Weights:
        def __init__(self, size):
            self.size = size
            self.per = heads_cols // size
            self.ref = weights4 if size == 4 else weights2

        def kind(self, other):
            return other if self.size == 4 else ((other + 1) // 2) % 2

        def column(self, other):
            return pl.ds(pl.multiple_of(self.kind(other) * self.per, self.per), self.per)

        def own_copies(self):
            return [
                pltpu.make_async_copy(
                    ref.at[:, self.column(y)],
                    self.ref.at[pl.ds(own_row, depth), pl.ds(j * self.per, self.per)],
                    local_sem.at[j],
                )
                for j, ref in enumerate(sources)
            ]

        def y_copies(self):
            out = []
            for n, other in enumerate(ring[1:]):
                for j, ref in enumerate(sources):
                    first, rows = 0, depth
                    if self.size == 2 and n > 0:
                        first, rows = pl.multiple_of(both_from, 16), BOTH
                    src = ref.at[pl.ds(first, rows), self.column(other)]
                    dst = self.ref.at[
                        pl.ds(pl.multiple_of(own_row + first, 16), rows),
                        pl.ds(j * self.per, self.per),
                    ]
                    out.append(remote(src, dst, y_send.at[n, j], y_recv.at[n, j], at_y(other)))
            return out

        def rows(self, zz, part):
            if self.size == 4:
                return pl.ds(pl.multiple_of(zz * slab + part * pair, pair), pair)
            if part == 0:
                return pl.ds(pl.multiple_of(zz * slab + (y // 2) * pair, pair), pair)
            return pl.ds(pl.multiple_of(zz * slab + (1 - y // 2) * pair + KEEP, 16), 2 * BOTH)

        def z_copy(self, way, step, part, arrival=False):
            ahead = step + 1 if arrival else step
            zz = (z + NZ - ahead) % NZ if way == 0 else (z + ahead) % NZ
            ref = self.ref.at[self.rows(zz, part)]
            to = (z + 1) % NZ if way == 0 else (z + NZ - 1) % NZ
            return remote(
                ref,
                ref,
                z_send.at[way, step, part],
                z_recv.at[way, step, part],
                where(sec, tp, to * NY + y),
            )

        def f_copies(self, slot, zz):
            if self.size == 4:
                return []
            base = zz * slab + (y // 2) * pair
            out = []
            for h, start in enumerate((base, base + pair - KEEP)):
                ref = self.ref.at[pl.ds(pl.multiple_of(start, 16), KEEP)]
                out.append(
                    remote(ref, ref, f_send.at[slot, h], f_recv.at[slot, h], at_y(y_twin))
                )
            return out

        def start_y(self):
            for copy in self.y_copies():
                copy.start()

        def start_z(self):
            for copy in self.own_copies():
                copy.wait()
            for copy in self.y_copies():
                copy.wait_recv()
            for part in range(2):
                for way in range(2):
                    self.z_copy(way, 0, part).start()
            for copy in self.f_copies(0, z):
                copy.start()

        def relay(self, step):
            for part in range(2):
                for way in range(2):
                    if z_sent(way, step, part):
                        self.z_copy(way, step, part, arrival=True).wait_recv()
                        if z_sent(way, step + 1, part):
                            self.z_copy(way, step + 1, part).start()
                        if part == 0:
                            ahead = step + 1
                            zz = (z + NZ - ahead) % NZ if way == 0 else (z + ahead) % NZ
                            for copy in self.f_copies(1 + step + 4 * way, zz):
                                copy.start()

        def finish(self):
            for step in range(4):
                for part in range(2):
                    for way in range(2):
                        if z_sent(way, step, part):
                            self.z_copy(way, step, part).wait_send()
            for k in range(8):
                for copy in self.f_copies(k, z):
                    copy.wait()
            for copy in self.y_copies():
                copy.wait_send()

    def z_sent(way, step, part):
        return step < 3 or (step == 3 and part == way)

    def each(condition, action):
        @pl.when(condition & wide)
        def _():
            action(Weights(4))

        @pl.when(condition & (sec >= 2))
        def _():
            action(Weights(2))

    slot = tp * NY + y
    peers = [(t, other) for t in (tp, 1 - tp) for other in ring][1:]

    def first_copy(n, w):
        t, other = peers[n]
        ref = blocks.at[w, tp, y]
        return remote(
            ref, ref, tok_send.at[0, w, n], x_recv.at[w, slot], where(sec, t, z * NY + other)
        )

    def token_copy(n, w):
        t, other = peers[n]
        ref = blocks.at[WAVES + w, tp, y, pl.ds(M, L)]
        return remote(
            ref, ref, tok_send.at[1, w, n], tok_recv.at[w, slot], where(sec, t, z * NY + other)
        )

    def part_copy(s):
        index = jnp.maximum(sec - 1, 0)
        return remote(
            parts.at[NSEC - 1, s], parts.at[index, s], part_send.at[s], part_recv.at[index, s], where(0, tp, doc)
        )

    def len_copy(n, arrival=False):
        index = ring[n + 1] if arrival else y
        ref = lens.at[index]
        return remote(ref, ref, len_send.at[n], len_recv.at[n], at_y(ring[n + 1]))


    small_copies = [
        pltpu.make_async_copy(len_hbm, len_ref, local_sem.at[4]),
        pltpu.make_async_copy(mix_hbm, mix_ref, local_sem.at[5]),
        pltpu.make_async_copy(ids_hbm, ids_ref, local_sem.at[6]),
        pltpu.make_async_copy(mem_hbm, mem_ref, local_sem.at[7]),
        pltpu.make_async_copy(gain_hbm.at[:, pl.ds(0, width)], gain_ref.at[0], local_sem.at[8]),
        pltpu.make_async_copy(gain_hbm.at[:, pl.ds(width, width)], gain_ref.at[1], local_sem.at[9]),
    ]
    table_copy = pltpu.make_async_copy(table_hbm, table, local_sem.at[10])
    wo_copy = pltpu.make_async_copy(wo_ref, w_out, local_sem.at[3])
    for copy in small_copies:
        copy.start()
    for group in (Weights(4), Weights(2)):

        @pl.when(wide if group.size == 4 else sec >= 2)
        def _():
            for copy in group.own_copies():
                copy.start()


    next_sec = (sec + 1) % NSEC
    last_sec = (sec + NSEC - 1) % NSEC
    greeted = [where(sec, t, z * NY + other) for t, other in peers]
    greeted += [where(sec, tp, (z + step) % NZ * NY + y) for step in (1, NZ - 1)]
    greeted += [
        where(to, t, z * NY + other)
        for to in (next_sec, last_sec)
        for t in (tp, 1 - tp)
        for other in ring
    ]
    greeted += [where((sec + 2) % NSEC, tp, doc)]
    barrier = pltpu.get_barrier_semaphore()
    for to in greeted:
        pl.semaphore_signal(barrier, inc=1, device_id=to, device_id_type=pl.DeviceIdType.MESH)
    pl.semaphore_wait(barrier, len(greeted))

    each(sec >= 0, Weights.start_y)
    table_copy.start()
    wo_copy.start()
    for copy in small_copies:
        copy.wait()

    lane = lax.broadcasted_iota(jnp.int32, (1, 128), 1)
    mine = (lane >= bit * ROWS) & (lane < bit * ROWS + ROWS)
    for t in range(SEGS * WAVES):
        lens[y, t : t + 1, :] = jnp.where(mine, len_ref[t % WAVES, t // WAVES], 0)
    for t in range(SEGS * WAVES, 8):
        lens[y, t : t + 1, :] = jnp.zeros((1, 128), jnp.int32)
    for n in range(3):
        len_copy(n).start()

    even = sec % 2 == 0
    odd = sec % 2 == 1
    each(even, Weights.start_z)

    n_ids = SEGS * WAVES * L
    eye = lax.broadcasted_iota(jnp.int32, (L, L), 0) == lax.broadcasted_iota(jnp.int32, (L, L), 1)
    columns = [
        jnp.sum(
            jnp.where(eye, ids_ref[w, s : s + 1, :].astype(jnp.float32), 0.0), -1, keepdims=True
        )
        for s in range(SEGS)
        for w in range(WAVES)
    ]
    wanted = jnp.concatenate(columns, axis=0).astype(jnp.int32) - sec * table.shape[0]
    for k in range(0, table.shape[0], 512):
        place = lax.broadcasted_iota(jnp.int32, (n_ids, 512), 1) + k
        picks[:, k : k + 512] = jnp.where(place == wanted, 1.0, 0.0).astype(jnp.bfloat16)
    each(even, lambda group: group.relay(0))
    table_copy.wait()

    def pick(j, carry):
        cols = pl.ds(pl.multiple_of(j * 512, 512), 512)
        rows = jnp.dot(picks[...], table[:, cols], preferred_element_type=jnp.float32)
        parts[NSEC - 1, :, :, :, cols] = rows.astype(jnp.bfloat16).reshape(SEGS, WAVES, L, 512)
        return carry

    lax.fori_loop(0, width // 1024, pick, 0)
    each(even, lambda group: group.relay(1))
    lax.fori_loop(width // 1024, width // 512, pick, 0)

    @pl.when(sec > 0)
    def _():
        for s in range(SEGS):
            part_copy(s).start()

    each(even, lambda group: group.relay(2))

    @pl.when(even)
    def _():
        pl.semaphore_signal(
            go_sem, inc=1, device_id=where(sec + 1, tp, doc), device_id_type=pl.DeviceIdType.MESH
        )

    @pl.when(sec == 0)
    def _():
        for s in range(SEGS):
            for index in range(NSEC - 1):
                remote(
                    parts.at[NSEC - 1, s],
                    parts.at[index, s],
                    part_send.at[s],
                    part_recv.at[index, s],
                    where(1, tp, doc),
                ).wait_recv()
            for w in range(WAVES):
                rows = parts[0, s, w] + parts[1, s, w] + parts[2, s, w] + parts[3, s, w]
                blocks[s * WAVES + w, tp, y, M:, :] = rows
                if s == 0:
                    blocks[w, tp, y, :M, :] = mem_ref[...]
            for w in range(WAVES):
                for n in range(7):
                    (first_copy if s == 0 else token_copy)(n, w).start()

    @pl.when(odd)
    def _():
        pl.semaphore_wait(go_sem, 1)

    def late(group):
        group.start_z()
        for step in range(3):
            group.relay(step)

    each(odd, late)
    each(sec >= 0, lambda group: group.relay(3))
    each(sec >= 0, Weights.finish)
    wo_copy.wait()
    for n in range(3):
        len_copy(n).wait_send()
        len_copy(n, arrival=True).wait_recv()

    near = sec % 2 == 0

    def members(size):
        return ring if size == 4 else ring[:2]

    def b_copy(t, n, size):
        to_tp = tp if n < size else 1 - tp
        other = members(size)[n % size]
        return remote(
            result.at[t],
            blocks.at[t, tp, y],
            x_send.at[t, n],
            x_recv.at[t, slot],
            where((sec + 1) % NSEC, to_tp, z * NY + other),
        )

    def h_copy(t, n):
        return remote(
            result.at[t],
            blocks.at[t, tp, y],
            x_send.at[t, n],
            x_recv.at[t, slot],
            where((sec + 1) % NSEC, 1 - tp, z * NY + ring[n]),
        )

    def m_copy(t, n):
        return remote(
            result.at[t, pl.ds(0, M)],
            blocks.at[t + WAVES, tp, y, pl.ds(0, M)],
            x_send.at[t, n],
            x_recv.at[t + WAVES, slot],
            where(0, 1 - tp, z * NY + ring[n]),
        )

    def forward(t, n, rows):
        ref = blocks.at[t, 1 - tp, ring[n], rows]
        return remote(
            ref, ref, r_send.at[t, n], x_recv.at[t, (1 - tp) * NY + ring[n]], where(sec, 1 - tp, doc)
        )

    def arrival(t, half, other, rows, tokens=False):
        ref = blocks.at[t, half, other, rows]
        source = half * NY + other
        sem = tok_recv.at[t - WAVES, source] if tokens else x_recv.at[t, source]
        return remote(ref, ref, x_send.at[0, 0], sem, at_y(y_mate))

    def head_cols(size, t, other):
        per = heads_cols // size
        start = t * heads_cols + Weights(size).kind(other) * per
        return pl.ds(pl.multiple_of(start, per), per)

    def a_peers(size):
        return [(t, other) for t in (tp, 1 - tp) for other in members(size)][1:]

    def mixed_rows(size, t, other):
        return mixed4.at[t, other] if size == 4 else mixed2.at[t, other % 2]

    def a_copy(t, n, size):
        to_tp, other = a_peers(size)[n]
        return remote(
            mixed_rows(size, t, other),
            heads.at[t, :, head_cols(size, tp, y)],
            a_send.at[t, n],
            a_recv.at[t, slot],
            where(sec, to_tp, z * NY + other),
        )

    def a_arrival(t, n, size):
        from_tp, other = a_peers(size)[n]
        return remote(
            mixed_rows(size, t, other),
            heads.at[t, :, head_cols(size, from_tp, other)],
            a_send.at[t, n],
            a_recv.at[t, from_tp * NY + other],
            at_y(y_mate),
        )

    def pool_copy(w):
        index = jnp.minimum(sec, NSEC - 2)
        return remote(
            pool.at[w], pool_in.at[index, w], pool_send.at[w], pool_recv.at[index, w], where(NSEC - 1, tp, doc)
        )

    def total_copy(w, to):
        return remote(
            total.at[w], cast, total_send.at[w, to // 2], total_recv, where(to, tp, doc)
        )

    all_rows = pl.ds(0, ROWS)
    scale = 1.0 / math.sqrt(HD)

    def attend(t, size):
        s = t // WAVES
        per = heads_cols // size
        docs = members(size)
        n_rows = size * ROWS
        group = Weights(size)
        far = near & ((sec > 0) | (s == 1))
        first = jnp.where(far, 1 - tp, tp)

        def wait_half(n):
            half = first if n == 0 else 1 - first

            @pl.when(odd)
            def _():
                for other in docs:
                    arrival(t, half, other, all_rows).wait_recv()

            if size == 2:

                @pl.when(even)
                def _():
                    for k, other in enumerate(docs):
                        arrival(t, half, other, all_rows).wait_recv()
                        if n == 0:
                            forward(t, k, all_rows).start()

                return

            @pl.when(even & (s == 0))
            def _():
                for other in docs[1 - n :]:
                    arrival(t, half, other, all_rows).wait_recv()

            @pl.when(even & (s == 1))
            def _():
                for other in docs[n:]:
                    arrival(t, half, other, pl.ds(M, L), tokens=True).wait_recv()
                for k, other in enumerate(docs):
                    arrival(t, half, other, pl.ds(0, M)).wait_recv()
                    if n == 0:
                        forward(t, k, pl.ds(0, M)).start()

        step = 128
        total_sum = sum2 if size == 2 else sum4
        qkv = qkv2 if size == 2 else qkv4
        base = pl.multiple_of(y // 2 * 2, 2) if size == 2 else 0
        square = jnp.zeros((n_rows, step), jnp.float32)
        for n in range(2):
            half = first if n == 0 else 1 - first
            wait_half(n)
            for c in range(0, width, step):
                x = blocks[t, half, pl.ds(base, size), :, c : c + step]
                x = x.reshape(n_rows, step).astype(jnp.float32)
                square = square + x * x
                scaled[:n_rows, c : c + step] = (x * gain_ref[half, :, c : c + step]).astype(
                    jnp.bfloat16
                )
            if n == 1:
                mean_square = jnp.sum(square, -1, keepdims=True) * (1.0 / (2 * width))
                inverse = lax.rsqrt(mean_square + EPSILON)
            rows = pl.ds(pl.multiple_of(half * width, width), width)

            def project(j, carry):
                cols = pl.ds(pl.multiple_of(j * per, per), per)
                out = jnp.dot(
                    scaled[:n_rows, :], group.ref[rows, cols], preferred_element_type=jnp.float32
                )
                if n == 0:
                    total_sum[j] = out
                else:
                    qkv[j] = ((total_sum[j] + out) * inverse).astype(jnp.bfloat16)
                return carry

            lax.fori_loop(0, 3, project, 0)

        shape = (2 * ROWS, 2 * ROWS)
        row = lax.broadcasted_iota(jnp.int32, shape, 0)
        col = lax.broadcasted_iota(jnp.int32, shape, 1)
        row_doc = (row >= ROWS).astype(jnp.int32)
        col_doc = (col >= ROWS).astype(jnp.int32)
        i = row - ROWS * row_doc
        j = col - ROWS * col_doc
        ordered = (row_doc == col_doc) & ((j < M) | (i < M) | (j <= i))
        for p in range(size // 2):
            d = base + 2 * p
            lengths = (lens[d, pl.ds(t, 1), :] + lens[d + 1, pl.ds(t, 1), :])[:, : 2 * ROWS]
            allowed = ordered & ((j < M) | (j - M < lengths))
            own = slice(p * 2 * ROWS, (p + 1) * 2 * ROWS)
            for h in range(per // HD):
                cols = slice(h * HD, (h + 1) * HD)
                scores = (
                    lax.dot_general(
                        qkv[0, own, cols],
                        qkv[1, own, cols],
                        (((1,), (1,)), ((), ())),
                        preferred_element_type=jnp.float32,
                    )
                    * scale
                )
                scores = jnp.where(allowed, scores, NEGATIVE)
                exps = jnp.where(allowed, jnp.exp(scores), 0.0)
                probs = (exps / jnp.sum(exps, -1, keepdims=True)).astype(jnp.bfloat16)
                out = jnp.dot(probs, qkv[2, own, cols], preferred_element_type=jnp.float32)
                out = out.astype(jnp.bfloat16).reshape(2, ROWS, HD)
                if size == 4:
                    mixed4[t, 2 * p : 2 * p + 2, :, cols] = out
                else:
                    mixed2[t, :, :, cols] = out

        count = 2 * size - 1
        for n in range(count):
            a_copy(t, n, size).start()
        heads[t, :, head_cols(size, tp, y)] = mixed4[t, y] if size == 4 else mixed2[t, bit]
        for n in range(count):
            a_arrival(t, n, size).wait_recv()

    def task(t, carry):
        s = t // WAVES
        w = t % WAVES

        @pl.when(wide)
        def _():
            attend(t, 4)

        @pl.when(sec >= 2)
        def _():
            attend(t, 2)

        length = len_ref[w, s]
        position = lax.broadcasted_iota(jnp.int32, (ROWS, 1), 0)
        token_ok = (position >= M) & (position - M < length)
        factor = mix_ref[0] / length.astype(jnp.float32)

        def finish(j, carry):
            cols = pl.ds(pl.multiple_of(j * 512, 512), 512)
            update = jnp.dot(heads[t], w_out[:, cols], preferred_element_type=jnp.float32)
            out = (blocks[t, tp, y, :, cols].astype(jnp.float32) + update).astype(jnp.bfloat16)
            result[t, :, cols] = out
            summed = jnp.sum(jnp.where(token_ok, out.astype(jnp.float32), 0.0), 0, keepdims=True)
            pool_row[:, cols] = summed * factor
            return carry

        lax.fori_loop(0, width // 512, finish, 0)

        @pl.when(sec == 0)
        def _():
            for n in range(8):
                b_copy(t, n, 4).start()

        @pl.when(sec == 2)
        def _():
            for n in range(4):
                b_copy(t, n, 2).start()

        @pl.when(sec == 1)
        def _():
            for n in range(2):
                h_copy(t, n).start()

        @pl.when((sec == NSEC - 1) & (s == 0))
        def _():
            for n in range(4):
                m_copy(t, n).start()

        @pl.when(s == 1)
        def _():
            for k in range(width // 128):
                pool[w, k : k + 1, :] = pool_row[:, k * 128 : (k + 1) * 128]

            @pl.when(sec < NSEC - 1)
            def _():
                pool_copy(w).start()

            @pl.when(sec == NSEC - 1)
            def _():
                for index in range(NSEC - 1):
                    remote(
                        pool.at[w],
                        pool_in.at[index, w],
                        pool_send.at[w],
                        pool_recv.at[index, w],
                        where(0, tp, doc),
                    ).wait_recv()
                summed = pool[w] + pool_in[0, w] + pool_in[1, w] + pool_in[2, w]
                total[w] = summed

                @pl.when(w == 0)
                def _():
                    total_copy(0, 0).start()
                    total_copy(0, 2).start()

                @pl.when(w == 1)
                def _():
                    total_copy(1, 1).start()
                    cast[...] = summed

        return carry

    lax.fori_loop(0, SEGS * WAVES, task, 0)

    core = sec % 2
    base = sec - core
    n_docs = NY * NZ

    @pl.when(sec < NSEC - 1)
    def _():
        remote(
            total.at[0], cast, total_send.at[0, 0], total_recv, where(NSEC - 1, tp, doc)
        ).wait_recv()

    def cast_copy(k, which):
        to = base + core if which == 0 else base + 1 - core
        return remote(
            cast,
            out_ref.at[2 * doc + core],
            cast_send.at[which, k],
            cast_recv.at[core, doc],
            where(to, tp, (doc + k) % n_docs),
        )

    cast_copy(0, 1).start()

    def send_row(k, carry):
        cast_copy(k, 0).start()
        cast_copy(k, 1).start()
        return carry

    lax.fori_loop(1, n_docs, send_row, 0)
    out_ref[2 * doc + core] = cast[...]

    def row_arrival(c, d):
        return remote(
            cast, out_ref.at[2 * d + c], cast_send.at[0, 0], cast_recv.at[c, d], where(base + 1 - core, tp, doc)
        )

    row_arrival(1 - core, doc).wait_recv()

    def take_row(k, carry):
        d = (doc + k) % n_docs
        row_arrival(core, d).wait_recv()
        row_arrival(1 - core, d).wait_recv()
        return carry

    lax.fori_loop(1, n_docs, take_row, 0)

    cast_copy(0, 1).wait_send()

    def sent_row(k, carry):
        cast_copy(k, 0).wait_send()
        cast_copy(k, 1).wait_send()
        return carry

    lax.fori_loop(1, n_docs, sent_row, 0)

    @pl.when(sec > 0)
    def _():
        for s in range(SEGS):
            part_copy(s).wait_send()

    @pl.when(sec == 0)
    def _():
        for w in range(WAVES):
            for n in range(7):
                first_copy(n, w).wait_send()
                token_copy(n, w).wait_send()

    def sent_task(t, carry):
        @pl.when(wide)
        def _():
            for n in range(7):
                a_copy(t, n, 4).wait_send()

        @pl.when(sec >= 2)
        def _():
            for n in range(3):
                a_copy(t, n, 2).wait_send()

        @pl.when(sec == 0)
        def _():
            for n in range(8):
                b_copy(t, n, 4).wait_send()

        @pl.when(sec == 2)
        def _():
            for n in range(4):
                b_copy(t, n, 2).wait_send()

        @pl.when(sec == 1)
        def _():
            for n in range(2):
                h_copy(t, n).wait_send()

        @pl.when((sec == NSEC - 1) & (t < WAVES))
        def _():
            for n in range(4):
                m_copy(t, n).wait_send()

        @pl.when(sec == 2)
        def _():
            for n in range(2):
                forward(t, n, all_rows).wait_send()

        @pl.when((sec == 0) & (t >= WAVES))
        def _():
            for n in range(4):
                forward(t, n, pl.ds(0, M)).wait_send()

        return carry

    lax.fori_loop(0, SEGS * WAVES, sent_task, 0)

    @pl.when(sec < NSEC - 1)
    def _():
        for w in range(WAVES):
            pool_copy(w).wait_send()

    @pl.when(sec == NSEC - 1)
    def _():
        total_copy(0, 0).wait_send()
        total_copy(0, 2).wait_send()
        total_copy(1, 1).wait_send()


def body(
    token_ids,
    seg_lengths,
    emb_table,
    mem_init,
    norm_gain,
    w_query,
    w_key,
    w_value,
    w_out,
    layer_mix,
):
    doc_local = token_ids.shape[0]
    vocab_rows, width = emb_table.shape
    depth, head_cols = w_query.shape[1:]
    half, quarter = head_cols // 2, head_cols // 4
    n_tasks = SEGS * WAVES
    dma = pltpu.SemaphoreType.DMA
    bf16, f32 = jnp.bfloat16, jnp.float32
    any_space = pl.BlockSpec(memory_space=pl.ANY)
    vmem = pl.BlockSpec(memory_space=pltpu.VMEM)
    lanes = width // 128
    rows = pl.pallas_call(
        kernel,
        out_shape=jax.ShapeDtypeStruct((NY * NZ * WAVES, lanes, 128), f32),
        in_specs=[any_space] * 10,
        out_specs=vmem,
        scratch_shapes=[
            pltpu.VMEM((WAVES, SEGS, L), jnp.int32),
            pltpu.VMEM((vocab_rows, width), bf16),
            pltpu.VMEM((n_tasks * L, vocab_rows), bf16),
            pltpu.VMEM((M, width), bf16),
            pltpu.VMEM((2, 1, width), f32),
            pltpu.SMEM((doc_local, SEGS), jnp.int32),
            pltpu.SMEM((1,), f32),
            pltpu.VMEM((2 * width, 3 * half), bf16),
            pltpu.VMEM((2 * width, 3 * quarter), bf16),
            pltpu.VMEM((2 * head_cols, width), bf16),
            pltpu.VMEM((n_tasks, 2, NY, ROWS, width), bf16),
            pltpu.VMEM((4 * ROWS, width), bf16),
            pltpu.VMEM((3, 2 * ROWS, half), f32),
            pltpu.VMEM((3, 4 * ROWS, quarter), f32),
            pltpu.VMEM((3, 2 * ROWS, half), bf16),
            pltpu.VMEM((3, 4 * ROWS, quarter), bf16),
            pltpu.VMEM((n_tasks, 2, ROWS, half), bf16),
            pltpu.VMEM((n_tasks, 4, ROWS, quarter), bf16),
            pltpu.VMEM((n_tasks, ROWS, 2 * head_cols), bf16),
            pltpu.VMEM((n_tasks, ROWS, width), bf16),
            pltpu.VMEM((NSEC, SEGS, WAVES, L, width), bf16),
            pltpu.VMEM((NY, 8, 128), jnp.int32),
            pltpu.VMEM((1, width), f32),
            pltpu.VMEM((WAVES, lanes, 128), f32),
            pltpu.VMEM((NSEC - 1, WAVES, lanes, 128), f32),
            pltpu.VMEM((WAVES, lanes, 128), f32),
            pltpu.VMEM((lanes, 128), f32),
            dma((11,)),
            dma((3, 3)),
            dma((3, 3)),
            dma((2, 4, 2)),
            dma((2, 4, 2)),
            dma((8, 2)),
            dma((8, 2)),
            dma((3,)),
            dma((3,)),
            dma((SEGS,)),
            dma((NSEC - 1, SEGS)),
            dma((SEGS, WAVES, 7)),
            dma((WAVES, 8)),
            dma((n_tasks, 8)),
            dma((n_tasks, 8)),
            dma((n_tasks, 4)),
            dma((n_tasks, 7)),
            dma((n_tasks, 8)),
            dma((WAVES,)),
            dma((NSEC - 1, WAVES)),
            dma((WAVES, 2)),
            dma,
            dma((2, NY * NZ)),
            dma((2, NY * NZ)),
            pltpu.SemaphoreType.REGULAR,
        ],
        compiler_params=pltpu.CompilerParams(
            has_side_effects=True, collective_id=0, vmem_limit_bytes=67000000
        ),
    )(
        token_ids,
        emb_table,
        mem_init,
        norm_gain,
        seg_lengths,
        layer_mix,
        w_query[0],
        w_key[0],
        w_value[0],
        w_out[0],
    )
    return rows.reshape(NY * NZ * WAVES, width)


def solution(mesh):
    return jax.shard_map(
        body,
        mesh=mesh,
        in_specs=(
            P("doc", None, None),
            P("doc", None),
            P("section", "tp"),
            P(None, "tp"),
            P("section", None),
            P("section", "doc", "tp"),
            P("section", "doc", "tp"),
            P("section", "doc", "tp"),
            P("section", None, "tp"),
            P("section"),
        ),
        out_specs=P(None, "tp"),
        check_vma=False,
    )
```

time: 286 us -> 284 us (level)
  no operation moved by 1% of the time
where the time goes in v3:
time: 284 us
  Pallas kernels  281 us (99%)
    pallas_call x1, Pallas kernels, body(): pl.pallas_call(kernel, out_shape=jax.ShapeDtypeStruct((NY * NZ * WAVES, l...  281 us

profile of v3, /device:TPU:1, one launch (start us, length us, event | category | flops | bytes accessed | tf_op | source)
XLA Modules:
  0.0 284.0 jit_solution(14323841791294606081)
XLA Ops:
  0.7 281.3 %shard_map.100 = f32[64,16,128]{2,1,0:T(8,128)} custom-call(s32[2,2,32]{2,1,0:T(2,128)} %ids_hbm.1, bf16[4096,2048]{1,0:T(8,128)(2,1)} %table_hbm.1, bf16[16,2048]{1,0:T(8,128)(2,1)} %mem_hbm.1, f32[1,4096]{1,0:T(1,128)} %gain_hbm.1, s32[2,2]{1,0:T(2,128)} %len_hbm.1, f32[1]{0:T(128)S(6)} %copy.14.mix_hbm, bf16[128,1024]{1,0:T(8,128)(2,1)} %bitcast.10, ...), custom_call_target="tpu_custom_call" | custom-call | tf_op jit(solution)/shard_map/pallas_call | solution.py:846
  282.0 2.0 copy.13

commit v4 on v3

--- a/solution.py
+++ b/solution.py
@@ -17,8 +17,8 @@
 
 NY = 4
 NZ = 8
-KEEP = 80
-BOTH = 48
+KEEP_EARLY = 112
+KEEP_LATE = 80
 WAVES = 2
 NSEC = 4
 
@@ -120,15 +120,16 @@
     def at_y(other):
         return where(sec, tp, z * NY + other)
 
-    wide = sec < 2
+    wide = sec == 0
     ring = [y, y_mate, y_twin, y_far]
     sources = (wq_ref, wk_ref, wv_ref)
     own_row = pl.multiple_of(doc * depth, depth)
-    both_from = (1 - bit) * KEEP
 
     class Weights:
-        def __init__(self, size):
+        def __init__(self, size, keep=KEEP_LATE):
             self.size = size
+            self.keep = keep
+            self.both = depth - keep
             self.per = heads_cols // size
             self.ref = weights4 if size == 4 else weights2
 
@@ -154,7 +155,7 @@
                 for j, ref in enumerate(sources):
                     first, rows = 0, depth
                     if self.size == 2 and n > 0:
-                        first, rows = pl.multiple_of(both_from, 16), BOTH
+                        first, rows = pl.multiple_of((1 - bit) * self.keep, 16), self.both
                     src = ref.at[pl.ds(first, rows), self.column(other)]
                     dst = self.ref.at[
                         pl.ds(pl.multiple_of(own_row + first, 16), rows),
@@ -168,7 +169,7 @@
                 return pl.ds(pl.multiple_of(zz * slab + part * pair, pair), pair)
             if part == 0:
                 return pl.ds(pl.multiple_of(zz * slab + (y // 2) * pair, pair), pair)
-            return pl.ds(pl.multiple_of(zz * slab + (1 - y // 2) * pair + KEEP, 16), 2 * BOTH)
+            return pl.ds(pl.multiple_of(zz * slab + (1 - y // 2) * pair + self.keep, 16), 2 * self.both)
 
         def z_copy(self, way, step, part, arrival=False):
             ahead = step + 1 if arrival else step
@@ -188,8 +189,8 @@
                 return []
             base = zz * slab + (y // 2) * pair
             out = []
-            for h, start in enumerate((base, base + pair - KEEP)):
-                ref = self.ref.at[pl.ds(pl.multiple_of(start, 16), KEEP)]
+            for h, start in enumerate((base, base + pair - self.keep)):
+                ref = self.ref.at[pl.ds(pl.multiple_of(start, 16), self.keep)]
                 out.append(
                     remote(ref, ref, f_send.at[slot, h], f_recv.at[slot, h], at_y(y_twin))
                 )
@@ -242,6 +243,10 @@
         @pl.when(condition & wide)
         def _():
             action(Weights(4))
+
+        @pl.when(condition & (sec == 1))
+        def _():
+            action(Weights(2, KEEP_EARLY))
 
         @pl.when(condition & (sec >= 2))
         def _():
@@ -290,7 +295,7 @@
         copy.start()
     for group in (Weights(4), Weights(2)):
 
-        @pl.when(wide if group.size == 4 else sec >= 2)
+        @pl.when(wide if group.size == 4 else sec >= 1)
         def _():
             for copy in group.own_copies():
                 copy.start()
@@ -329,6 +334,7 @@
 
     even = sec % 2 == 0
     odd = sec % 2 == 1
+    urgent = sec == 0
     each(even, Weights.start_z)
 
     n_ids = SEGS * WAVES * L
@@ -344,7 +350,14 @@
     for k in range(0, table.shape[0], 512):
         place = lax.broadcasted_iota(jnp.int32, (n_ids, 512), 1) + k
         picks[:, k : k + 512] = jnp.where(place == wanted, 1.0, 0.0).astype(jnp.bfloat16)
-    each(even, lambda group: group.relay(0))
+    each(urgent, lambda group: group.relay(0))
+
+    def let_go():
+        pl.semaphore_signal(
+            go_sem, inc=1, device_id=where(sec + 1, tp, doc), device_id_type=pl.DeviceIdType.MESH
+        )
+
+    pl.when(urgent)(let_go)
     table_copy.wait()
 
     def pick(j, carry):
@@ -354,21 +367,13 @@
         return carry
 
     lax.fori_loop(0, width // 1024, pick, 0)
-    each(even, lambda group: group.relay(1))
+    each(urgent, lambda group: group.relay(1))
     lax.fori_loop(width // 1024, width // 512, pick, 0)
 
     @pl.when(sec > 0)
     def _():
         for s in range(SEGS):
             part_copy(s).start()
-
-    each(even, lambda group: group.relay(2))
-
-    @pl.when(even)
-    def _():
-        pl.semaphore_signal(
-            go_sem, inc=1, device_id=where(sec + 1, tp, doc), device_id_type=pl.DeviceIdType.MESH
-        )
 
     @pl.when(sec == 0)
     def _():
@@ -390,6 +395,15 @@
                 for n in range(7):
                     (first_copy if s == 0 else token_copy)(n, w).start()
 
+    each(urgent, lambda group: group.relay(2))
+
+    @pl.when(sec == 2)
+    def _():
+        group = Weights(2)
+        for step in range(3):
+            group.relay(step)
+        let_go()
+
     @pl.when(odd)
     def _():
         pl.semaphore_wait(go_sem, 1)
@@ -560,8 +574,8 @@
                 inverse = lax.rsqrt(mean_square + EPSILON)
             rows = pl.ds(pl.multiple_of(half * width, width), width)
 
-            def project(j, carry):
-                cols = pl.ds(pl.multiple_of(j * per, per), per)
+            for j in range(3):
+                cols = slice(j * per, (j + 1) * per)
                 out = jnp.dot(
                     scaled[:n_rows, :], group.ref[rows, cols], preferred_element_type=jnp.float32
                 )
@@ -569,9 +583,6 @@
                     total_sum[j] = out
                 else:
                     qkv[j] = ((total_sum[j] + out) * inverse).astype(jnp.bfloat16)
-                return carry
-
-            lax.fori_loop(0, 3, project, 0)
 
         shape = (2 * ROWS, 2 * ROWS)
         row = lax.broadcasted_iota(jnp.int32, shape, 0)
@@ -622,7 +633,7 @@
         def _():
             attend(t, 4)
 
-        @pl.when(sec >= 2)
+        @pl.when(sec >= 1)
         def _():
             attend(t, 2)
 
@@ -631,23 +642,15 @@
         token_ok = (position >= M) & (position - M < length)
         factor = mix_ref[0] / length.astype(jnp.float32)
 
-        def finish(j, carry):
-            cols = pl.ds(pl.multiple_of(j * 512, 512), 512)
+        for j in range(width // 512):
+            cols = slice(j * 512, (j + 1) * 512)
             update = jnp.dot(heads[t], w_out[:, cols], preferred_element_type=jnp.float32)
             out = (blocks[t, tp, y, :, cols].astype(jnp.float32) + update).astype(jnp.bfloat16)
             result[t, :, cols] = out
             summed = jnp.sum(jnp.where(token_ok, out.astype(jnp.float32), 0.0), 0, keepdims=True)
             pool_row[:, cols] = summed * factor
-            return carry
-
-        lax.fori_loop(0, width // 512, finish, 0)
-
-        @pl.when(sec == 0)
-        def _():
-            for n in range(8):
-                b_copy(t, n, 4).start()
-
-        @pl.when(sec == 2)
+
+        @pl.when(near)
         def _():
             for n in range(4):
                 b_copy(t, n, 2).start()
@@ -770,17 +773,12 @@
             for n in range(7):
                 a_copy(t, n, 4).wait_send()
 
-        @pl.when(sec >= 2)
+        @pl.when(sec >= 1)
         def _():
             for n in range(3):
                 a_copy(t, n, 2).wait_send()
 
-        @pl.when(sec == 0)
-        def _():
-            for n in range(8):
-                b_copy(t, n, 4).wait_send()
-
-        @pl.when(sec == 2)
+        @pl.when(near)
         def _():
             for n in range(4):
                 b_copy(t, n, 2).wait_send()

time: 284 us -> 285 us (level)
  no operation moved by 1% of the time
where the time goes in v4:
time: 285 us
  Pallas kernels  282 us (99%)
    pallas_call x1, Pallas kernels, body(): pl.pallas_call(kernel, out_shape=jax.ShapeDtypeStruct((NY * NZ * WAVES, l...  282 us

profile of v4, /device:TPU:1, one launch (start us, length us, event | category | flops | bytes accessed | tf_op | source)
XLA Modules:
  0.0 285.1 jit_solution(13009210956375241167)
XLA Ops:
  0.7 282.4 %shard_map.100 = f32[64,16,128]{2,1,0:T(8,128)} custom-call(s32[2,2,32]{2,1,0:T(2,128)} %ids_hbm.1, bf16[4096,2048]{1,0:T(8,128)(2,1)} %table_hbm.1, bf16[16,2048]{1,0:T(8,128)(2,1)} %mem_hbm.1, f32[1,4096]{1,0:T(1,128)} %gain_hbm.1, s32[2,2]{1,0:T(2,128)} %len_hbm.1, f32[1]{0:T(128)S(6)} %copy.14.mix_hbm, bf16[128,1024]{1,0:T(8,128)(2,1)} %bitcast.10, ...), custom_call_target="tpu_custom_call" | custom-call | tf_op jit(solution)/shard_map/pallas_call | solution.py:844
  283.1 2.0 copy.13

commit v5 on v4

--- a/solution.py
+++ b/solution.py
@@ -17,7 +17,7 @@
 
 NY = 4
 NZ = 8
-KEEP_EARLY = 112
+KEEP_EARLY = 96
 KEEP_LATE = 80
 WAVES = 2
 NSEC = 4
@@ -54,6 +54,7 @@
     mixed2,
     mixed4,
     heads,
+    update,
     result,
     parts,
     lens,
@@ -73,6 +74,7 @@
     len_recv,
     part_send,
     part_recv,
+    first_send,
     tok_send,
     tok_recv,
     x_send,
@@ -255,18 +257,23 @@
     slot = tp * NY + y
     peers = [(t, other) for t in (tp, 1 - tp) for other in ring][1:]
 
-    def first_copy(n, w):
+    part_width = width // 2
+
+    def part_cols(c):
+        return pl.ds(c * part_width, part_width)
+
+    def first_copy(n, w, c):
         t, other = peers[n]
-        ref = blocks.at[w, tp, y]
-        return remote(
-            ref, ref, tok_send.at[0, w, n], x_recv.at[w, slot], where(sec, t, z * NY + other)
+        ref = blocks.at[w, tp, y, :, part_cols(c)]
+        return remote(
+            ref, ref, first_send.at[w, n, c], x_recv.at[w, slot, c], where(sec, t, z * NY + other)
         )
 
     def token_copy(n, w):
         t, other = peers[n]
         ref = blocks.at[WAVES + w, tp, y, pl.ds(M, L)]
         return remote(
-            ref, ref, tok_send.at[1, w, n], tok_recv.at[w, slot], where(sec, t, z * NY + other)
+            ref, ref, tok_send.at[w, n], tok_recv.at[w, slot], where(sec, t, z * NY + other)
         )
 
     def part_copy(s):
@@ -334,8 +341,8 @@
 
     even = sec % 2 == 0
     odd = sec % 2 == 1
-    urgent = sec == 0
-    each(even, Weights.start_z)
+    urgent = sec < 2
+    each(sec <= 2, Weights.start_z)
 
     n_ids = SEGS * WAVES * L
     eye = lax.broadcasted_iota(jnp.int32, (L, L), 0) == lax.broadcasted_iota(jnp.int32, (L, L), 1)
@@ -350,14 +357,12 @@
     for k in range(0, table.shape[0], 512):
         place = lax.broadcasted_iota(jnp.int32, (n_ids, 512), 1) + k
         picks[:, k : k + 512] = jnp.where(place == wanted, 1.0, 0.0).astype(jnp.bfloat16)
-    each(urgent, lambda group: group.relay(0))
-
     def let_go():
         pl.semaphore_signal(
             go_sem, inc=1, device_id=where(sec + 1, tp, doc), device_id_type=pl.DeviceIdType.MESH
         )
 
-    pl.when(urgent)(let_go)
+    each(urgent, lambda group: group.relay(0))
     table_copy.wait()
 
     def pick(j, carry):
@@ -393,9 +398,15 @@
                     blocks[w, tp, y, :M, :] = mem_ref[...]
             for w in range(WAVES):
                 for n in range(7):
-                    (first_copy if s == 0 else token_copy)(n, w).start()
-
-    each(urgent, lambda group: group.relay(2))
+                    if s == 0:
+                        first_copy(n, w, 0).start()
+                        first_copy(n, w, 1).start()
+                    else:
+                        token_copy(n, w).start()
+
+    @pl.when(sec == 0)
+    def _():
+        Weights(4).relay(2)
 
     @pl.when(sec == 2)
     def _():
@@ -404,16 +415,18 @@
             group.relay(step)
         let_go()
 
-    @pl.when(odd)
+    @pl.when(sec == 1)
+    def _():
+        Weights(2, KEEP_EARLY).relay(2)
+
+    @pl.when(sec == 3)
     def _():
         pl.semaphore_wait(go_sem, 1)
-
-    def late(group):
+        group = Weights(2)
         group.start_z()
         for step in range(3):
             group.relay(step)
 
-    each(odd, late)
     each(sec >= 0, lambda group: group.relay(3))
     each(sec >= 0, Weights.finish)
     wo_copy.wait()
@@ -426,46 +439,53 @@
     def members(size):
         return ring if size == 4 else ring[:2]
 
-    def b_copy(t, n, size):
-        to_tp = tp if n < size else 1 - tp
-        other = members(size)[n % size]
-        return remote(
-            result.at[t],
-            blocks.at[t, tp, y],
-            x_send.at[t, n],
-            x_recv.at[t, slot],
-            where((sec + 1) % NSEC, to_tp, z * NY + other),
-        )
-
-    def h_copy(t, n):
-        return remote(
-            result.at[t],
-            blocks.at[t, tp, y],
-            x_send.at[t, n],
-            x_recv.at[t, slot],
+    def b_copy(t, n, c):
+        to_tp = tp if n < 2 else 1 - tp
+        return remote(
+            result.at[t, :, part_cols(c)],
+            blocks.at[t, tp, y, :, part_cols(c)],
+            x_send.at[t, n, c],
+            x_recv.at[t, slot, c],
+            where((sec + 1) % NSEC, to_tp, z * NY + ring[n % 2]),
+        )
+
+    def h_copy(t, n, c):
+        return remote(
+            result.at[t, :, part_cols(c)],
+            blocks.at[t, tp, y, :, part_cols(c)],
+            x_send.at[t, n, c],
+            x_recv.at[t, slot, c],
             where((sec + 1) % NSEC, 1 - tp, z * NY + ring[n]),
         )
 
-    def m_copy(t, n):
-        return remote(
-            result.at[t, pl.ds(0, M)],
-            blocks.at[t + WAVES, tp, y, pl.ds(0, M)],
-            x_send.at[t, n],
-            x_recv.at[t + WAVES, slot],
+    def m_copy(t, n, c):
+        return remote(
+            result.at[t, pl.ds(0, M), part_cols(c)],
+            blocks.at[t + WAVES, tp, y, pl.ds(0, M), part_cols(c)],
+            x_send.at[t, n, c],
+            x_recv.at[t + WAVES, slot, c],
             where(0, 1 - tp, z * NY + ring[n]),
         )
 
-    def forward(t, n, rows):
-        ref = blocks.at[t, 1 - tp, ring[n], rows]
-        return remote(
-            ref, ref, r_send.at[t, n], x_recv.at[t, (1 - tp) * NY + ring[n]], where(sec, 1 - tp, doc)
-        )
-
-    def arrival(t, half, other, rows, tokens=False):
-        ref = blocks.at[t, half, other, rows]
-        source = half * NY + other
-        sem = tok_recv.at[t - WAVES, source] if tokens else x_recv.at[t, source]
-        return remote(ref, ref, x_send.at[0, 0], sem, at_y(y_mate))
+    def forward(t, n, rows, c):
+        ref = blocks.at[t, 1 - tp, ring[n], rows, part_cols(c)]
+        return remote(
+            ref,
+            ref,
+            r_send.at[t, n, c],
+            x_recv.at[t, (1 - tp) * NY + ring[n], c],
+            where(sec, 1 - tp, doc),
+        )
+
+    def arrival(t, half, other, rows, c):
+        ref = blocks.at[t, half, other, rows, part_cols(c)]
+        sem = x_recv.at[t, half * NY + other, c]
+        return remote(ref, ref, x_send.at[0, 0, 0], sem, at_y(y_mate))
+
+    def token_arrival(t, half, other):
+        ref = blocks.at[t, half, other, pl.ds(M, L)]
+        sem = tok_recv.at[t - WAVES, half * NY + other]
+        return remote(ref, ref, x_send.at[0, 0, 0], sem, at_y(y_mate))
 
     def head_cols(size, t, other):
         per = heads_cols // size
@@ -524,35 +544,34 @@
         def wait_half(n):
             half = first if n == 0 else 1 - first
 
+            def take(others, rows, onward):
+                for c in range(2):
+                    for k, other in enumerate(others):
+                        arrival(t, half, other, rows, c).wait_recv()
+                        if onward:
+                            forward(t, k, rows, c).start()
+
             @pl.when(odd)
             def _():
-                for other in docs:
-                    arrival(t, half, other, all_rows).wait_recv()
+                take(docs, all_rows, False)
 
             if size == 2:
 
                 @pl.when(even)
                 def _():
-                    for k, other in enumerate(docs):
-                        arrival(t, half, other, all_rows).wait_recv()
-                        if n == 0:
-                            forward(t, k, all_rows).start()
+                    take(docs, all_rows, n == 0)
 
                 return
 
             @pl.when(even & (s == 0))
             def _():
-                for other in docs[1 - n :]:
-                    arrival(t, half, other, all_rows).wait_recv()
+                take(docs[1 - n :], all_rows, False)
 
             @pl.when(even & (s == 1))
             def _():
                 for other in docs[n:]:
-                    arrival(t, half, other, pl.ds(M, L), tokens=True).wait_recv()
-                for k, other in enumerate(docs):
-                    arrival(t, half, other, pl.ds(0, M)).wait_recv()
-                    if n == 0:
-                        forward(t, k, pl.ds(0, M)).start()
+                    token_arrival(t, half, other).wait_recv()
+                take(docs, pl.ds(0, M), n == 0)
 
         step = 128
         total_sum = sum2 if size == 2 else sum4
@@ -622,48 +641,61 @@
         for n in range(count):
             a_copy(t, n, size).start()
         heads[t, :, head_cols(size, tp, y)] = mixed4[t, y] if size == 4 else mixed2[t, bit]
+        update[...] = jnp.zeros_like(update)
+        where_from = [(tp, y)] + a_peers(size)
         for n in range(count):
+            own = head_cols(size, *where_from[n])
+            update[...] += jnp.dot(
+                heads[t, :, own], w_out[own, :], preferred_element_type=jnp.float32
+            )
             a_arrival(t, n, size).wait_recv()
-
-    def task(t, carry):
-        s = t // WAVES
+        last = head_cols(size, *where_from[count])
+
         w = t % WAVES
-
-        @pl.when(wide)
-        def _():
-            attend(t, 4)
-
-        @pl.when(sec >= 1)
-        def _():
-            attend(t, 2)
-
         length = len_ref[w, s]
         position = lax.broadcasted_iota(jnp.int32, (ROWS, 1), 0)
         token_ok = (position >= M) & (position - M < length)
         factor = mix_ref[0] / length.astype(jnp.float32)
 
-        for j in range(width // 512):
-            cols = slice(j * 512, (j + 1) * 512)
-            update = jnp.dot(heads[t], w_out[:, cols], preferred_element_type=jnp.float32)
-            out = (blocks[t, tp, y, :, cols].astype(jnp.float32) + update).astype(jnp.bfloat16)
-            result[t, :, cols] = out
-            summed = jnp.sum(jnp.where(token_ok, out.astype(jnp.float32), 0.0), 0, keepdims=True)
-            pool_row[:, cols] = summed * factor
-
-        @pl.when(near)
-        def _():
-            for n in range(4):
-                b_copy(t, n, 2).start()
-
-        @pl.when(sec == 1)
-        def _():
-            for n in range(2):
-                h_copy(t, n).start()
-
-        @pl.when((sec == NSEC - 1) & (s == 0))
-        def _():
-            for n in range(4):
-                m_copy(t, n).start()
+        for c in range(2):
+            for k in range(0, part_width, 512):
+                cols = slice(c * part_width + k, c * part_width + k + 512)
+                out = update[:, cols] + jnp.dot(
+                    heads[t, :, last], w_out[last, cols], preferred_element_type=jnp.float32
+                )
+                out = (blocks[t, tp, y, :, cols].astype(jnp.float32) + out).astype(jnp.bfloat16)
+                result[t, :, cols] = out
+                summed = jnp.where(token_ok, out.astype(jnp.float32), 0.0)
+                pool_row[:, cols] = jnp.sum(summed, 0, keepdims=True) * factor
+
+            @pl.when(near)
+            def _():
+                for n in range(4):
+                    b_copy(t, n, c).start()
+
+            if size == 2:
+
+                @pl.when(sec == 1)
+                def _():
+                    for n in range(2):
+                        h_copy(t, n, c).start()
+
+                @pl.when((sec == NSEC - 1) & (s == 0))
+                def _():
+                    for n in range(4):
+                        m_copy(t, n, c).start()
+
+    def task(t, carry):
+        s = t // WAVES
+        w = t % WAVES
+
+        @pl.when(wide)
+        def _():
+            attend(t, 4)
+
+        @pl.when(sec >= 1)
+        def _():
+            attend(t, 2)
 
         @pl.when(s == 1)
         def _():
@@ -764,7 +796,8 @@
     def _():
         for w in range(WAVES):
             for n in range(7):
-                first_copy(n, w).wait_send()
+                first_copy(n, w, 0).wait_send()
+                first_copy(n, w, 1).wait_send()
                 token_copy(n, w).wait_send()
 
     def sent_task(t, carry):
@@ -781,27 +814,32 @@
         @pl.when(near)
         def _():
             for n in range(4):
-                b_copy(t, n, 2).wait_send()
+                b_copy(t, n, 0).wait_send()
+                b_copy(t, n, 1).wait_send()
 
         @pl.when(sec == 1)
         def _():
             for n in range(2):
-                h_copy(t, n).wait_send()
+                h_copy(t, n, 0).wait_send()
+                h_copy(t, n, 1).wait_send()
 
         @pl.when((sec == NSEC - 1) & (t < WAVES))
         def _():
             for n in range(4):
-                m_copy(t, n).wait_send()
+                m_copy(t, n, 0).wait_send()
+                m_copy(t, n, 1).wait_send()
 
         @pl.when(sec == 2)
         def _():
             for n in range(2):
-                forward(t, n, all_rows).wait_send()
+                forward(t, n, all_rows, 0).wait_send()
+                forward(t, n, all_rows, 1).wait_send()
 
         @pl.when((sec == 0) & (t >= WAVES))
         def _():
             for n in range(4):
-                forward(t, n, pl.ds(0, M)).wait_send()
+                forward(t, n, pl.ds(0, M), 0).wait_send()
+                forward(t, n, pl.ds(0, M), 1).wait_send()
 
         return carry
 
@@ -866,6 +904,7 @@
             pltpu.VMEM((n_tasks, 2, ROWS, half), bf16),
             pltpu.VMEM((n_tasks, 4, ROWS, quarter), bf16),
             pltpu.VMEM((n_tasks, ROWS, 2 * head_cols), bf16),
+            pltpu.VMEM((ROWS, width), f32),
             pltpu.VMEM((n_tasks, ROWS, width), bf16),
             pltpu.VMEM((NSEC, SEGS, WAVES, L, width), bf16),
             pltpu.VMEM((NY, 8, 128), jnp.int32),
@@ -885,11 +924,12 @@
             dma((3,)),
             dma((SEGS,)),
             dma((NSEC - 1, SEGS)),
-            dma((SEGS, WAVES, 7)),
+            dma((WAVES, 7, 2)),
+            dma((WAVES, 7)),
             dma((WAVES, 8)),
-            dma((n_tasks, 8)),
-            dma((n_tasks, 8)),
-            dma((n_tasks, 4)),
+            dma((n_tasks, 4, 2)),
+            dma((n_tasks, 8, 2)),
+            dma((n_tasks, 4, 2)),
             dma((n_tasks, 7)),
             dma((n_tasks, 8)),
             dma((WAVES,)),

time: 285 us -> 269 us (0.944)
  Pallas kernels: 282 us -> 266 us
    pallas_call x1, Pallas kernels: 282 us -> 266 us  [body(): pl.pallas_call(kernel, out_shape=jax.ShapeDtypeStruct((NY * NZ * WAVES, l...]
where the time goes in v5:
time: 269 us
  Pallas kernels  266 us (99%)
    pallas_call x1, Pallas kernels, body(): pl.pallas_call(kernel, out_shape=jax.ShapeDtypeStruct((NY * NZ * WAVES, l...  266 us

profile of v5, /device:TPU:1, one launch (start us, length us, event | category | flops | bytes accessed | tf_op | source)
XLA Modules:
  0.0 269.0 jit_solution(13627866866276440320)
XLA Ops:
  0.7 266.3 %shard_map.100 = f32[64,16,128]{2,1,0:T(8,128)} custom-call(s32[2,2,32]{2,1,0:T(2,128)} %ids_hbm.1, bf16[4096,2048]{1,0:T(8,128)(2,1)} %table_hbm.1, bf16[16,2048]{1,0:T(8,128)(2,1)} %mem_hbm.1, f32[1,4096]{1,0:T(1,128)} %gain_hbm.1, s32[2,2]{1,0:T(2,128)} %len_hbm.1, f32[1]{0:T(128)S(6)} %copy.14.mix_hbm, bf16[128,1024]{1,0:T(8,128)(2,1)} %bitcast.10, ...), custom_call_target="tpu_custom_call" | custom-call | tf_op jit(solution)/shard_map/pallas_call | solution.py:882
  267.0 2.0 copy.13

commit v6 on v5

--- a/solution.py
+++ b/solution.py
@@ -326,7 +326,6 @@
 
     each(sec >= 0, Weights.start_y)
     table_copy.start()
-    wo_copy.start()
     for copy in small_copies:
         copy.wait()
 
@@ -364,6 +363,7 @@
 
     each(urgent, lambda group: group.relay(0))
     table_copy.wait()
+    wo_copy.start()
 
     def pick(j, carry):
         cols = pl.ds(pl.multiple_of(j * 512, 512), 512)
@@ -401,8 +401,6 @@
                     if s == 0:
                         first_copy(n, w, 0).start()
                         first_copy(n, w, 1).start()
-                    else:
-                        token_copy(n, w).start()
 
     @pl.when(sec == 0)
     def _():
@@ -638,7 +636,7 @@
                     mixed2[t, :, :, cols] = out
 
         count = 2 * size - 1
-        for n in range(count):
+        for n in reversed(range(count)):
             a_copy(t, n, size).start()
         heads[t, :, head_cols(size, tp, y)] = mixed4[t, y] if size == 4 else mixed2[t, bit]
         update[...] = jnp.zeros_like(update)
@@ -670,7 +668,7 @@
 
             @pl.when(near)
             def _():
-                for n in range(4):
+                for n in (3, 2, 1, 0):
                     b_copy(t, n, c).start()
 
             if size == 2:
@@ -696,6 +694,12 @@
         @pl.when(sec >= 1)
         def _():
             attend(t, 2)
+
+        @pl.when((sec == 0) & (t == WAVES - 1))
+        def _():
+            for document in range(WAVES):
+                for n in range(7):
+                    token_copy(n, document).start()
 
         @pl.when(s == 1)
         def _():

time: 269 us -> 266 us (0.989)
  Pallas kernels: 266 us -> 263 us
    pallas_call x1, Pallas kernels: 266 us -> 263 us  [body(): pl.pallas_call(kernel, out_shape=jax.ShapeDtypeStruct((NY * NZ * WAVES, l...]
where the time goes in v6:
time: 266 us
  Pallas kernels  263 us (99%)
    pallas_call x1, Pallas kernels, body(): pl.pallas_call(kernel, out_shape=jax.ShapeDtypeStruct((NY * NZ * WAVES, l...  263 us

profile of v6, /device:TPU:1, one launch (start us, length us, event | category | flops | bytes accessed | tf_op | source)
XLA Modules:
  0.0 265.7 jit_solution(14728846254560474366)
XLA Ops:
  0.7 263.1 %shard_map.100 = f32[64,16,128]{2,1,0:T(8,128)} custom-call(s32[2,2,32]{2,1,0:T(2,128)} %ids_hbm.1, bf16[4096,2048]{1,0:T(8,128)(2,1)} %table_hbm.1, bf16[16,2048]{1,0:T(8,128)(2,1)} %mem_hbm.1, f32[1,4096]{1,0:T(1,128)} %gain_hbm.1, s32[2,2]{1,0:T(2,128)} %len_hbm.1, f32[1]{0:T(128)S(6)} %copy.14.mix_hbm, bf16[128,1024]{1,0:T(8,128)(2,1)} %bitcast.10, ...), custom_call_target="tpu_custom_call" | custom-call | tf_op jit(solution)/shard_map/pallas_call | solution.py:886
  263.7 2.0 copy.13

commit v7 on v6

--- a/solution.py
+++ b/solution.py
@@ -639,6 +639,10 @@
         for n in reversed(range(count)):
             a_copy(t, n, size).start()
         heads[t, :, head_cols(size, tp, y)] = mixed4[t, y] if size == 4 else mixed2[t, bit]
+
+    def output(t, size):
+        s = t // WAVES
+        count = 2 * size - 1
         update[...] = jnp.zeros_like(update)
         where_from = [(tp, y)] + a_peers(size)
         for n in range(count):
@@ -683,17 +687,28 @@
                     for n in range(4):
                         m_copy(t, n, c).start()
 
-    def task(t, carry):
+    def mix(t, carry):
+        @pl.when(wide)
+        def _():
+            attend(t, 4)
+
+        @pl.when(sec >= 1)
+        def _():
+            attend(t, 2)
+
+        return carry
+
+    def close(t, carry):
         s = t // WAVES
         w = t % WAVES
 
         @pl.when(wide)
         def _():
-            attend(t, 4)
+            output(t, 4)
 
         @pl.when(sec >= 1)
         def _():
-            attend(t, 2)
+            output(t, 2)
 
         @pl.when((sec == 0) & (t == WAVES - 1))
         def _():
@@ -735,7 +750,12 @@
 
         return carry
 
-    lax.fori_loop(0, SEGS * WAVES, task, 0)
+    def segment(s, carry):
+        lax.fori_loop(s * WAVES, (s + 1) * WAVES, mix, 0)
+        lax.fori_loop(s * WAVES, (s + 1) * WAVES, close, 0)
+        return carry
+
+    lax.fori_loop(0, SEGS, segment, 0)
 
     core = sec % 2
     base = sec - core

time: 266 us -> 279 us (1.049)
  Pallas kernels: 263 us -> 276 us
    pallas_call x1, Pallas kernels: 263 us -> 276 us  [body(): pl.pallas_call(kernel, out_shape=jax.ShapeDtypeStruct((NY * NZ * WAVES, l...]
where the time goes in v7:
time: 279 us; the launch traced here: 278 us
  Pallas kernels  276 us (99%)
    pallas_call x1, Pallas kernels, body(): pl.pallas_call(kernel, out_shape=jax.ShapeDtypeStruct((NY * NZ * WAVES, l...  276 us

profile of v7, /device:TPU:1, one launch (start us, length us, event | category | flops | bytes accessed | tf_op | source)
XLA Modules:
  0.0 278.4 jit_solution(7170018111890567871)
XLA Ops:
  0.7 275.8 %shard_map.100 = f32[64,16,128]{2,1,0:T(8,128)} custom-call(s32[2,2,32]{2,1,0:T(2,128)} %ids_hbm.1, bf16[4096,2048]{1,0:T(8,128)(2,1)} %table_hbm.1, bf16[16,2048]{1,0:T(8,128)(2,1)} %mem_hbm.1, f32[1,4096]{1,0:T(1,128)} %gain_hbm.1, s32[2,2]{1,0:T(2,128)} %len_hbm.1, f32[1]{0:T(128)S(6)} %copy.14.mix_hbm, bf16[128,1024]{1,0:T(8,128)(2,1)} %bitcast.10, ...), custom_call_target="tpu_custom_call" | custom-call | tf_op jit(solution)/shard_map/pallas_call | solution.py:906
  276.4 2.0 copy.13

commit v8 on v6

--- a/solution.py
+++ b/solution.py
@@ -639,13 +639,11 @@
         for n in reversed(range(count)):
             a_copy(t, n, size).start()
         heads[t, :, head_cols(size, tp, y)] = mixed4[t, y] if size == 4 else mixed2[t, bit]
-        update[...] = jnp.zeros_like(update)
         where_from = [(tp, y)] + a_peers(size)
         for n in range(count):
             own = head_cols(size, *where_from[n])
-            update[...] += jnp.dot(
-                heads[t, :, own], w_out[own, :], preferred_element_type=jnp.float32
-            )
+            product = jnp.dot(heads[t, :, own], w_out[own, :], preferred_element_type=jnp.float32)
+            update[...] = product if n == 0 else update[...] + product
             a_arrival(t, n, size).wait_recv()
         last = head_cols(size, *where_from[count])
 
@@ -764,7 +762,10 @@
         cast_copy(k, 1).start()
         return carry
 
-    lax.fori_loop(1, n_docs, send_row, 0)
+    far = n_docs // 2
+    lax.fori_loop(far - NY, far + NY + 1, send_row, 0)
+    lax.fori_loop(1, far - NY, send_row, 0)
+    lax.fori_loop(far + NY + 1, n_docs, send_row, 0)
     out_ref[2 * doc + core] = cast[...]
 
     def row_arrival(c, d):

time: 266 us -> 266 us (level)
  no operation moved by 1% of the time
where the time goes in v8:
time: 266 us
  Pallas kernels  263 us (99%)
    pallas_call x1, Pallas kernels, body(): pl.pallas_call(kernel, out_shape=jax.ShapeDtypeStruct((NY * NZ * WAVES, l...  263 us

profile of v8, /device:TPU:1, one launch (start us, length us, event | category | flops | bytes accessed | tf_op | source)
XLA Modules:
  0.0 266.0 jit_solution(1581841198343002482)
XLA Ops:
  0.7 263.3 %shard_map.100 = f32[64,16,128]{2,1,0:T(8,128)} custom-call(s32[2,2,32]{2,1,0:T(2,128)} %ids_hbm.1, bf16[4096,2048]{1,0:T(8,128)(2,1)} %table_hbm.1, bf16[16,2048]{1,0:T(8,128)(2,1)} %mem_hbm.1, f32[1,4096]{1,0:T(1,128)} %gain_hbm.1, s32[2,2]{1,0:T(2,128)} %len_hbm.1, f32[1]{0:T(128)S(6)} %copy.14.mix_hbm, bf16[128,1024]{1,0:T(8,128)(2,1)} %bitcast.10, ...), custom_call_target="tpu_custom_call" | custom-call | tf_op jit(solution)/shard_map/pallas_call | solution.py:887
  264.0 2.0 copy.13
